TPU v7x, 256 devices: a whole 4x4x8 slice. The times are simulated.
256 devices in a mesh: tm: 16 (over y_hi, z), sub: 16 (over x, y_lo, core).
Axes of the slice: x: 4, y: 4 (y_hi: 2, y_lo: 2; y = y_hi * 2 + y_lo), z: 8, core: 2. Of those that a mesh axis runs over, the one named last changes fastest.
Arguments:
- frames: bfloat16 [16384, 1024], P(('tm', 'sub')), may hold values from -16 to 16
- modulation: float32 [8, 1024], replicated, may hold values from -4 to 4
- w_project: bfloat16 [3, 1024, 1024], P(None, None, 'sub'), may hold values from -1 to 1
- w_heads_out: bfloat16 [1024, 1024], P('sub'), may hold values from -0.25 to 0.25
- w_up: bfloat16 [1024, 4096], P(None, 'sub'), may hold values from -0.1875 to 0.1875
- w_down: bfloat16 [4096, 1024], P('sub'), may hold values from -0.125 to 0.125
- w_velocity: bfloat16 [1024, 100], replicated, may hold values from -0.1875 to 0.1875
- noisy_mel: float32 [16384, 100], P('tm'), may hold values from -6 to 6
- w_prelude: bfloat16 [7, 1536, 100], P(None, 'sub'), may hold values from -0.21875 to 0.21875
- w_upsample: bfloat16 [8, 1536, 768], P(None, 'sub'), may hold values from -0.109375 to 0.109375
- snake_alpha: float32 [2, 768], replicated, may hold values from 0.3 to 3
- w_dilated: bfloat16 [3, 768, 768], P(None, 'sub'), may hold values from -0.125 to 0.125
- w_plain: bfloat16 [3, 768, 768], P(None, 'sub'), may hold values from -0.125 to 0.125
Outputs:
- mel_next: float32 [16384, 100], P('tm')
- section_out: bfloat16 [65536, 768], P(('tm', 'sub'))
All inputs are finite; a program needn't handle non-finite values.
Results may differ from a plain program's by a relative error of at most 0.03.
Values may be sent and summed in bfloat16 or wider, within the bound.
No kernel may reach another device: no remote copies, remote signals or barrier semaphores. Data moves between devices by JAX's collectives and lax.ppermute only.
A program may use at most 64 MiB of HBM per device.

v0:
```python
import math

import jax
import jax.numpy as jnp
from jax import lax
from jax.experimental import pallas as pl
from jax.experimental.pallas import tpu as pltpu
from jax.sharding import PartitionSpec as P


HEAD_DIM = 64
BLK = 256
MEL_PAD = 128
OFFSETS = 9

epsilon = 1e-06
bf16 = jnp.bfloat16
f32 = jnp.float32


def norm_rows(rows, offset_row, scale_row):
    rows = rows.astype(f32)
    center = jnp.mean(rows, axis=-1, keepdims=True)
    square = jnp.mean(rows * rows, axis=-1, keepdims=True)
    spread = square - center * center
    return (rows - center) * lax.rsqrt(spread + epsilon) * (1.0 + scale_row) + offset_row


def mm(a, b):
    return jnp.dot(a, b, preferred_element_type=f32)


def mm_t(a, b):
    return lax.dot_general(a, b, (((1,), (1,)), ((), ())), preferred_element_type=f32)


def vmem_specs(n):
    return [pl.BlockSpec(memory_space=pltpu.VMEM)] * n


def whole(kernel, out_shapes, args, scratch=(), cost=None, smem=0, vmem=24):
    single = not isinstance(out_shapes, (tuple, list))
    return pl.pallas_call(
        kernel,
        out_shape=out_shapes,
        in_specs=[pl.BlockSpec(memory_space=pltpu.SMEM)] * smem + vmem_specs(len(args) - smem),
        out_specs=vmem_specs(1)[0] if single else vmem_specs(len(out_shapes)),
        scratch_shapes=list(scratch),
        compiler_params=pltpu.CompilerParams(vmem_limit_bytes=vmem << 20),
        cost_estimate=cost,
    )(*args)


def cost_of(flops, nbytes, trans=0):
    return pl.CostEstimate(flops=flops, bytes_accessed=nbytes, transcendentals=trans)


def first_weights_kernel(
    w_ref, o_ref, pre_ref, dil_ref, plain_ref, a_ref, b_ref, voc_ref, pre_scratch, sems
):
    moves = (
        (w_ref.at[0], a_ref.at[pl.ds(0, 64), :]),
        (w_ref.at[1], a_ref.at[pl.ds(64, 64), :]),
        (w_ref.at[2], b_ref.at[pl.ds(0, 64), :]),
        (o_ref, b_ref.at[pl.ds(64, 64), :]),
        (dil_ref, voc_ref.at[pl.ds(96, 144), :]),
        (plain_ref, voc_ref.at[pl.ds(240, 144), :]),
        (pre_ref, pre_scratch),
    )
    copies = [pltpu.make_async_copy(src, dst, sems.at[n]) for n, (src, dst) in enumerate(moves)]
    for copy in copies:
        copy.start()
    voc_ref[0:96, :] = jnp.zeros((96, 768), bf16)
    copies[6].wait()
    for k in range(7):
        voc_ref[0:96, 100 * k : 100 * k + 100] = pre_scratch[k]
    for copy in copies[:6]:
        copy.wait()


def mlp_weights_kernel(up_ref, down_ref, out_ref):
    out_ref[0:1024, :] = up_ref[...]
    for k in range(4):
        out_ref[1024 + 256 * k : 1280 + 256 * k, :] = down_ref[:, 256 * k : 256 * k + 256]


TAP_ORDER = (2, 3, 4, 5, 6, 7, 0, 1)


def upsample_weights_kernel(w_ref, out_ref):
    def half(g, carry):
        lanes = pl.ds(pl.multiple_of(384 * g, 384), 384)
        for t, tap in enumerate(TAP_ORDER):
            rows = w_ref[tap, :, lanes]
            for i in range(8):
                out_ref[8 * g + i, :, 48 * t : 48 * t + 48] = rows[:, 48 * i : 48 * i + 48]
        return carry

    lax.fori_loop(0, 2, half, 0)


def attention_kernel(flag_ref, mod_ref, *refs):
    row_refs, weight_refs = refs[:8], refs[8:16]
    o0, o1, o2, o3, rows, w_a, w_v, w_out, heads, sems = refs[16:]
    copies = []
    for n, ref in enumerate(row_refs):
        copies.append((ref, rows.at[pl.ds(64 * n, 64), :]))
    for h in range(4):
        first_half, second_half = weight_refs[2 * h], weight_refs[2 * h + 1]
        copies.append((first_half, w_a.at[h]))
        copies.append((second_half.at[pl.ds(0, 64), :], w_v.at[h]))
        copies.append((second_half.at[pl.ds(64, 64), :], w_out.at[pl.ds(64 * h, 64), :]))
    copies = [pltpu.make_async_copy(src, dst, sems.at[n]) for n, (src, dst) in enumerate(copies)]
    for copy in copies:
        copy.start()
    first = flag_ref[0] > 0
    scale = 1.0 / math.sqrt(HEAD_DIM)
    for copy in copies[:8]:
        copy.wait()
    normed = norm_rows(rows[...], mod_ref[0:1, :], mod_ref[1:2, :]).astype(bf16)
    own, back = normed[:BLK], normed[BLK:]
    for copy in copies[8:]:
        copy.wait()

    def one_head(h):
        qk = mm_t(own, w_a[h]).astype(bf16)
        q, k = qk[:, 0:64], qk[:, 64:128]
        v = mm_t(own, w_v[h]).astype(bf16)
        kb = mm_t(back, w_a[h, 64:128, :]).astype(bf16)
        vb = mm_t(back, w_v[h]).astype(bf16)
        s_own = mm_t(q, k) * scale
        s_back = mm_t(q, kb) * scale
        s_back = jnp.where(first, -1e30, s_back)
        top = jnp.maximum(
            jnp.max(s_own, axis=-1, keepdims=True), jnp.max(s_back, axis=-1, keepdims=True)
        )
        e_own = jnp.exp(s_own - top)
        e_back = jnp.exp(s_back - top)
        total = jnp.sum(e_own, axis=-1, keepdims=True) + jnp.sum(e_back, axis=-1, keepdims=True)
        inv = 1.0 / total
        p_own = (e_own * inv).astype(bf16)
        p_back = (e_back * inv).astype(bf16)
        heads[h] = (mm(p_own, v) + mm(p_back, vb)).astype(bf16)

    lax.fori_loop(0, 4, lambda h, c: (one_head(h), c)[1], 0)
    outs = jnp.concatenate([heads[h] for h in range(4)], axis=1)
    total = mm(outs, w_out[...]).astype(bf16)
    for k, out in enumerate((o0, o1, o2, o3)):
        out[...] = total[64 * k : 64 * k + 64]


def sum_of(p0, p1, p2, p3):
    return (p0[...].astype(f32) + p1[...].astype(f32)) + (p2[...].astype(f32) + p3[...].astype(f32))


def after_attention_kernel(p0, p1, p2, p3, frames_ref, mod_ref, mixed_ref, norm_ref):
    attn = sum_of(p0, p1, p2, p3)
    mixed = (frames_ref[...].astype(f32) + mod_ref[2:3, :] * attn).astype(bf16)
    mixed_ref[...] = mixed
    norm_ref[...] = norm_rows(mixed, mod_ref[3:4, :], mod_ref[4:5, :]).astype(bf16)


def mlp_kernel(h0, h1, h2, h3, w0, w1, w2, w3, o0, o1, o2, o3, acc):
    h = jnp.concatenate([h0[...], h1[...], h2[...], h3[...]], axis=0)
    for i, w in enumerate((w0, w1, w2, w3)):
        up = mm(h, w[0:1024, :])
        hid = jax.nn.gelu(up, approximate=True).astype(bf16)
        for k in range(4):
            part = mm(hid, w[1024 + 256 * k : 1280 + 256 * k, :])
            cols = slice(256 * k, 256 * k + 256)
            if i == 0:
                acc[:, cols] = part
            elif i < 3:
                acc[:, cols] += part
            else:
                value = (acc[:, cols] + part).astype(bf16)
                for n, out in enumerate((o0, o1, o2, o3)):
                    out[:, cols] = value[64 * n : 64 * n + 64]


def after_mlp_kernel(p0, p1, p2, p3, mixed_ref, mod_ref, wv_ref, noisy_ref, out_ref):
    feed = sum_of(p0, p1, p2, p3)
    final = (mixed_ref[...].astype(f32) + mod_ref[5:6, :] * feed).astype(bf16)
    normed = norm_rows(final, mod_ref[6:7, :], mod_ref[7:8, :]).astype(bf16)
    mel = noisy_ref[...] + 0.5 * mm(normed, wv_ref[...])
    for s in range(16):
        out_ref[s] = mel


def placed_kernel(comp_ref, full_ref, here_ref):
    earlier = lax.broadcasted_iota(jnp.int32, (100, 192), 1) < 96
    full_ref[...] = jnp.zeros(full_ref.shape, bf16)
    here_ref[...] = jnp.zeros(here_ref.shape, bf16)
    here = [comp_ref[100 * j : 100 * j + 100, 0:192] for j in range(7)]
    near = [comp_ref[100 * j : 100 * j + 100, 192:384] for j in range(7)]
    for d in range(OFFSETS):
        value = jnp.zeros((100, 192), f32)
        if 0 <= d - 1 < 7:
            value = here[d - 1]
            here_ref[MEL_PAD * d : MEL_PAD * d + 100, :] = value.astype(bf16)
        if d < 7:
            value = value + jnp.where(earlier, near[d], 0.0)
        if 0 <= d - 2 < 7:
            value = value + jnp.where(earlier, 0.0, near[d - 2])
        full_ref[MEL_PAD * d : MEL_PAD * d + 100, :] = value.astype(bf16)


EXT = 1056


def upsample_kernel(flag_ref, mel_ref, before_ref, after_ref, full_ref, here_ref, out_ref, ext, up):
    ext[...] = jnp.zeros((EXT, MEL_PAD), f32)
    ext[0:8, 0:100] = before_ref[...]
    for s in range(16):
        ext[8 + 64 * s : 72 + 64 * s, 0:100] = mel_ref[s]
    ext[1032:1040, 0:100] = after_ref[...]
    cols = [ext[3 + k : 3 + k + 1032, :].astype(bf16) for k in range(OFFSETS)]
    up[...] = mm(jnp.concatenate(cols, axis=1), full_ref[...])
    earlier = lax.broadcasted_iota(jnp.int32, (8, 192), 1) < 96
    row = lax.broadcasted_iota(jnp.int32, (8, 192), 0)
    for which, base, r in ((0, 0, 1), (1, 1024, 0)):
        edge_cols = [ext[base + 3 + k : base + 11 + k, :].astype(bf16) for k in range(OFFSETS)]
        edge = mm(jnp.concatenate(edge_cols, axis=1), here_ref[...])
        lanes = earlier if which == 0 else jnp.logical_not(earlier)
        use = (flag_ref[which] > 0) & (row == r) & lanes
        up[base : base + 8, :] = jnp.where(use, edge, up[base : base + 8, :])
    for s in range(16):
        out_ref[s] = up[64 * s : 64 * s + ROWS, :].astype(bf16)


PI_PARTS = (3.140625, 0.000965118408203125, 2.5331974029541016e-06, 1.984187258941006e-09)


def sin_squared(x):
    k = jnp.round(x * (1.0 / math.pi))
    r = x
    for part in PI_PARTS:
        r = r - k * part
    z = r * r
    poly = -2.3889859e-08 * z + 2.7525562e-06
    poly = poly * z - 1.9840874e-04
    poly = poly * z + 8.3333310e-03
    poly = poly * z - 1.6666667e-01
    sine = r + r * (z * poly)
    return sine * sine


def snake_act(values, alpha_row, inverse_row):
    return values + sin_squared(alpha_row * values) * inverse_row


def shifted(plane, by):
    return pltpu.roll(plane, by % plane.shape[0], 0)


ROWS = 72


X_STEPS = (0, 3, 1, 2)


def shard_of(place_ref, which, step):
    return ((place_ref[0] + X_STEPS[step]) & 3) * 4 + (place_ref[1] ^ which)


def merge_kernel(own, left, right, far_top, far_bottom, pre_ref, dil_ref, plain_ref, sems):
    moves = []
    for n, ref in enumerate((own, left, right)):
        moves.append((ref.at[pl.ds(0, 96), :], pre_ref.at[n]))
        moves.append((ref.at[pl.ds(96, 144), :], dil_ref.at[n]))
        moves.append((ref.at[pl.ds(240, 144), :], plain_ref.at[n]))
    moves.append((far_top.at[pl.ds(0, 96), :], pre_ref.at[3]))
    moves.append((far_top.at[pl.ds(96, 144), :], dil_ref.at[3]))
    moves.append((far_bottom, plain_ref.at[3]))
    copies = [pltpu.make_async_copy(src, dst, sems.at[n]) for n, (src, dst) in enumerate(moves)]
    for copy in copies:
        copy.start()
    for copy in copies:
        copy.wait()


def prelude_weights_kernel(place_ref, p0, p1, p2, p3, out_ref, sems):
    copies = [
        pltpu.make_async_copy(
            ref.at[step], out_ref.at[shard_of(place_ref, which, step)], sems.at[which, step]
        )
        for which, ref in enumerate((p0, p1, p2, p3))
        for step in range(4)
    ]
    for copy in copies:
        copy.start()
    for copy in copies:
        copy.wait()


STRIDE = 80


def conv_kernel(flag_ref, place_ref, up_ref, alpha_ref, *refs):
    out_ref, planes, act_one, act_two, w_one, w_two, sems = refs[8:]
    copies = [
        [
            pltpu.make_async_copy(
                refs[4 * k + which].at[step],
                buf.at[shard_of(place_ref, which, step)],
                sems.at[k, which, step],
            )
            for which in range(4)
            for step in range(4)
        ]
        for k, buf in enumerate((w_one, w_two))
    ]
    for half in copies:
        for copy in half:
            copy.start()
    first = flag_ref[0] > 0
    last = flag_ref[1] > 0
    row = lax.broadcasted_iota(jnp.int32, (ROWS, 256), 0)
    outside = (first & (row == 0)) | (last & (row == 65))

    def gather_channels(g, carry):
        lanes = pl.ds(pl.multiple_of(384 * g, 384), 384)
        for p in range(4):
            parts = [up_ref[8 * g + i, :, 48 * p : 48 * p + 48] for i in range(8)]
            planes[p, :, lanes] = jnp.concatenate(parts, axis=1)
        return carry

    lax.fori_loop(0, 2, gather_channels, 0)
    act_one[...] = jnp.zeros(act_one.shape, bf16)
    act_two[...] = jnp.zeros(act_two.shape, bf16)

    def columns(n):
        return pl.ds(pl.multiple_of(256 * n, 256), 256)

    def up_plane(p, cols):
        return jnp.where(outside, 0.0, planes[p, :, cols].astype(f32))

    def products(act_ref, w_ref, cols):
        act = act_ref[...]
        y = []
        for tap in range(3):
            weight = jnp.concatenate(
                [w_ref[s, 48 * tap : 48 * tap + 48, cols] for s in range(16)], axis=0
            )
            v = mm(act, weight)
            y.append([v[STRIDE * p : STRIDE * p + ROWS] for p in range(4)])
        return y

    def first_act(n, carry):
        cols = columns(n)
        alpha = alpha_ref[0:1, cols]
        for p in range(4):
            value = snake_act(up_plane(p, cols), alpha, 1.0 / alpha).astype(bf16)
            act_one[STRIDE * p : STRIDE * p + ROWS, cols] = value
        return carry

    def first_conv(n, carry):
        cols = columns(n)
        alpha = alpha_ref[1:2, cols]
        y = products(act_one, w_one, cols)
        for p in range(4):
            before = y[0][0] if p == 3 else shifted(y[0][p + 1], 1)
            after = y[2][3] if p == 0 else shifted(y[2][p - 1], -1)
            value = snake_act(before + y[1][p] + after, alpha, 1.0 / alpha)
            value = jnp.where(outside, 0.0, value).astype(bf16)
            act_two[STRIDE * p : STRIDE * p + ROWS, cols] = value
        return carry

    def second_conv(n, carry):
        cols = columns(n)
        y = products(act_two, w_two, cols)
        for p in range(4):
            before = y[0][p - 1] if p >= 1 else shifted(y[0][3], 1)
            after = y[2][p + 1] if p <= 2 else shifted(y[2][0], -1)
            total = up_plane(p, cols) + (before + y[1][p] + after)
            to = pl.ds(pl.multiple_of(768 * p + 256 * n, 256), 256)
            out_ref[:, to] = shifted(total, -1)[0:64].astype(bf16)
        return carry

    lax.fori_loop(0, 3, first_act, 0)
    for copy in copies[0]:
        copy.wait()
    lax.fori_loop(0, 3, first_conv, 0)
    for copy in copies[1]:
        copy.wait()
    lax.fori_loop(0, 3, second_conv, 0)


def exchange(value, groups=None, axis="sub"):
    return lax.all_to_all(value, axis, 0, 0, tiled=True, axis_index_groups=groups)


def device(y_hi, z, x, y_lo, core):
    return (y_hi * 8 + z) * 16 + x * 4 + y_lo * 2 + core


OTHER_Y = [
    (device(h, z, x, y, c), device(1 - h, z, x, 1 - y, c))
    for h in range(2)
    for z in range(8)
    for x in range(4)
    for y in range(2)
    for c in range(2)
]
OTHER_GROUPS = [
    [device(y ^ side, z, x, y, c) for x in range(4) for y in range(2) for c in range(2)]
    for side in range(2)
    for z in range(8)
]


def program(
    frames,
    modulation,
    w_project,
    w_heads_out,
    w_up,
    w_down,
    w_velocity,
    noisy_mel,
    w_prelude,
    w_upsample,
    snake_alpha,
    w_dilated,
    w_plain,
):
    own_rows = frames.shape[0]
    sub_index = lax.axis_index("sub")
    time_index = lax.axis_index("tm")
    n_sub = lax.axis_size("sub")
    n_tm = lax.axis_size("tm")
    n_all = n_sub * n_tm
    both = ("tm", "sub")
    shape = jax.ShapeDtypeStruct
    here_index = time_index * n_sub + sub_index

    to_right = [(i, (i + 4) % 16) for i in range(16)]
    to_left = [(i, (i - 4) % 16) for i in range(16)]
    own_a, own_b, w_voc = pl.pallas_call(
        first_weights_kernel,
        out_shape=(shape((128, 1024), bf16), shape((128, 1024), bf16), shape((384, 768), bf16)),
        in_specs=[pl.BlockSpec(memory_space=pl.ANY)] * 5,
        out_specs=vmem_specs(3),
        scratch_shapes=[pltpu.VMEM((7, 96, 100), bf16), pltpu.SemaphoreType.DMA((7,))],
        compiler_params=pltpu.CompilerParams(vmem_limit_bytes=60 << 20),
        cost_estimate=cost_of(0, 3 << 20),
        name="first_weights",
    )(
        jnp.swapaxes(w_project, 1, 2),
        w_heads_out,
        w_prelude,
        w_dilated.reshape(144, 768),
        w_plain.reshape(144, 768),
    )
    back_frames = lax.ppermute(frames, both, [(i, i + 4) for i in range(n_all - 4)])
    left_a = lax.ppermute(own_a, "sub", to_right)
    right_b = lax.ppermute(own_b, "sub", to_left)
    left_b = lax.ppermute(own_b, "sub", to_right)
    right_a = lax.ppermute(own_a, "sub", to_left)
    far_a = lax.ppermute(left_a, "sub", to_right)
    far_b = lax.ppermute(right_b, "sub", to_left)

    voc_left = lax.ppermute(w_voc, "sub", to_right)
    voc_right = lax.ppermute(w_voc, "sub", to_left)
    voc_top = lax.ppermute(voc_left[:240], "sub", to_right)
    voc_bottom = lax.ppermute(voc_right[240:], "sub", to_left)
    pre_shape, conv_shape = shape((4, 96, 768), bf16), shape((4, 144, 768), bf16)
    raw = pl.BlockSpec(memory_space=pl.ANY)
    pre_own, dil_own, plain_own = pl.pallas_call(
        merge_kernel,
        out_shape=(pre_shape, conv_shape, conv_shape),
        in_specs=[raw] * 5,
        out_specs=vmem_specs(3),
        scratch_shapes=[pltpu.SemaphoreType.DMA((12,))],
        compiler_params=pltpu.CompilerParams(vmem_limit_bytes=60 << 20),
        cost_estimate=cost_of(0, 5 << 20),
        name="voc_merge",
    )(w_voc, voc_left, voc_right, voc_top, voc_bottom)
    beside = [[(i, i ^ k) for i in range(16)] for k in (1, 2, 3)]
    pre_y = lax.ppermute(pre_own, both, OTHER_Y)
    dil_y = lax.ppermute(dil_own, both, OTHER_Y)
    plain_y = lax.ppermute(plain_own, "sub", beside[1])
    pre_core = lax.ppermute(pre_own, "sub", beside[0])
    dil_core = lax.ppermute(dil_own, "sub", beside[0])
    plain_core = lax.ppermute(plain_own, "sub", beside[0])
    pre_both = lax.ppermute(pre_y, "sub", beside[0])
    dil_both = lax.ppermute(dil_y, "sub", beside[0])
    plain_both = lax.ppermute(plain_y, "sub", beside[0])
    place = jnp.stack([sub_index // 4, lax.rem(sub_index, 4)]).astype(jnp.int32)

    block = [frames] + [lax.ppermute(frames, "sub", beside[k - 1]) for k in (1, 2, 3)]
    back = [back_frames] + [lax.ppermute(back_frames, "sub", beside[k - 1]) for k in (1, 2, 3)]

    own_mlp = whole(
        mlp_weights_kernel, shape((2048, 256), bf16), (w_up, w_down), cost=cost_of(0, 2 << 20)
    )
    other_core = lax.ppermute(own_mlp, "sub", [(i, i ^ 1) for i in range(16)])
    other_y = lax.ppermute(own_mlp, both, OTHER_Y)
    other_both = lax.ppermute(other_y, "sub", [(i, i ^ 1) for i in range(16)])

    ups = whole(
        upsample_weights_kernel, shape((16, 96, 384), bf16), (w_upsample,), cost=cost_of(0, 3 << 20)
    )

    is_first = (time_index == 0) & (sub_index < 4)
    quarter = shape((own_rows, 1024), bf16)
    partial = pl.pallas_call(
        attention_kernel,
        out_shape=(quarter,) * 4,
        in_specs=[pl.BlockSpec(memory_space=pltpu.SMEM)]
        + vmem_specs(1)
        + [pl.BlockSpec(memory_space=pl.ANY)] * 16,
        out_specs=vmem_specs(4),
        scratch_shapes=[
            pltpu.VMEM((2 * BLK, 1024), bf16),
            pltpu.VMEM((4, 128, 1024), bf16),
            pltpu.VMEM((4, 64, 1024), bf16),
            pltpu.VMEM((256, 1024), bf16),
            pltpu.VMEM((4, BLK, 64), bf16),
            pltpu.SemaphoreType.DMA((20,)),
        ],
        compiler_params=pltpu.CompilerParams(vmem_limit_bytes=60 << 20),
        cost_estimate=cost_of(10**9, 4 << 20, 1 << 19),
        name="attention",
    )(
        is_first.astype(jnp.int32).reshape(1),
        modulation,
        *block,
        *back,
        own_a,
        own_b,
        left_a,
        left_b,
        right_a,
        right_b,
        far_a,
        far_b,
    )
    ups = exchange(ups, OTHER_GROUPS, both)
    parts = [partial[0]] + [lax.ppermute(partial[k], "sub", beside[k - 1]) for k in (1, 2, 3)]
    mixed_rows, own_norm = whole(
        after_attention_kernel,
        (quarter, quarter),
        (*parts, frames, modulation),
        cost=cost_of(10**6, 1 << 20),
    )

    own_norm, ups = lax.optimization_barrier((own_norm, ups))
    across = [(i, (i + 8) % 16) for i in range(16)]
    second = [
        own_norm,
        lax.ppermute(own_norm, "sub", across),
        lax.ppermute(own_norm, "sub", to_right),
        lax.ppermute(own_norm, "sub", to_left),
    ]
    partial = whole(
        mlp_kernel,
        (quarter,) * 4,
        (*second, own_mlp, other_core, other_y, other_both),
        scratch=[pltpu.VMEM((256, 1024), f32)],
        cost=cost_of(11 * 10**8, 5 << 20, 1 << 18),
    )
    parts = [
        partial[0],
        lax.ppermute(partial[1], "sub", across),
        lax.ppermute(partial[2], "sub", to_left),
        lax.ppermute(partial[3], "sub", to_right),
    ]
    noisy_own = lax.dynamic_slice_in_dim(noisy_mel, sub_index * own_rows, own_rows, 0)
    copies = whole(
        after_mlp_kernel,
        shape((16, own_rows, 100), f32),
        (*parts, mixed_rows, modulation, w_velocity, noisy_own),
        cost=cost_of(10**7, 1 << 20),
    )
    mel_all = exchange(copies)
    mel_next = mel_all.reshape(-1, 100)

    pre_all = pl.pallas_call(
        prelude_weights_kernel,
        out_shape=shape((16, 96, 768), bf16),
        in_specs=[pl.BlockSpec(memory_space=pltpu.SMEM)] + [raw] * 4,
        out_specs=pl.BlockSpec(memory_space=pltpu.VMEM),
        scratch_shapes=[pltpu.SemaphoreType.DMA((4, 4))],
        compiler_params=pltpu.CompilerParams(vmem_limit_bytes=60 << 20),
        cost_estimate=cost_of(0, 5 << 20),
        name="prelude_weights",
    )(place, pre_own, pre_core, pre_y, pre_both).reshape(1536, 768)
    comp = lax.dot_general(
        pre_all, ups.reshape(1536, 384), (((0,), (0,)), ((), ())), preferred_element_type=f32
    )
    w_full, w_here = whole(
        placed_kernel,
        (shape((OFFSETS * MEL_PAD, 192), bf16), shape((OFFSETS * MEL_PAD, 192), bf16)),
        (comp,),
        cost=cost_of(10**6, 2 << 20),
    )

    before = lax.ppermute(mel_all[15, 56:], "tm", [(i, i + 1) for i in range(n_tm - 1)])
    after = lax.ppermute(mel_all[0, :8], "tm", [(i + 1, i) for i in range(n_tm - 1)])
    windows = whole(
        upsample_kernel,
        shape((16, ROWS, 192), bf16),
        (
            jnp.stack([time_index == 0, time_index == n_tm - 1]).astype(jnp.int32),
            mel_all,
            before,
            after,
            w_full,
            w_here,
        ),
        scratch=[pltpu.VMEM((EXT, MEL_PAD), f32), pltpu.VMEM((1032, 192), f32)],
        cost=cost_of(5 * 10**8, 2 << 20),
        smem=1,
    )
    up_x = exchange(windows)

    flags = jnp.stack([here_index == 0, here_index == n_all - 1]).astype(jnp.int32)
    out = pl.pallas_call(
        conv_kernel,
        out_shape=shape((64, 3072), bf16),
        in_specs=[pl.BlockSpec(memory_space=pltpu.SMEM)] * 2 + vmem_specs(2) + [raw] * 8,
        out_specs=pl.BlockSpec(memory_space=pltpu.VMEM),
        scratch_shapes=[
            pltpu.VMEM((4, ROWS, 768), bf16),
            pltpu.VMEM((4 * STRIDE, 768), bf16),
            pltpu.VMEM((4 * STRIDE, 768), bf16),
            pltpu.VMEM((16, 144, 768), bf16),
            pltpu.VMEM((16, 144, 768), bf16),
            pltpu.SemaphoreType.DMA((2, 4, 4)),
        ],
        compiler_params=pltpu.CompilerParams(vmem_limit_bytes=60 << 20),
        cost_estimate=cost_of(2 * 10**9, 8 << 20, 1 << 18),
        name="convolutions",
    )(
        flags,
        place,
        up_x,
        snake_alpha,
        dil_own,
        dil_core,
        dil_y,
        dil_both,
        plain_own,
        plain_core,
        plain_y,
        plain_both,
    )
    return (mel_next, out.reshape(256, 768))


def solution(mesh):
    in_specs = (
        P(("tm", "sub"), None),
        P(),
        P(None, None, "sub"),
        P("sub", None),
        P(None, "sub"),
        P("sub", None),
        P(),
        P("tm", None),
        P(None, "sub", None),
        P(None, "sub", None),
        P(),
        P(None, "sub", None),
        P(None, "sub", None),
    )
    out_specs = (P("tm", None), P(("tm", "sub"), None))
    return jax.shard_map(program, mesh=mesh, in_specs=in_specs, out_specs=out_specs, check_vma=False)
```

profile of v0, /device:TPU:16, one launch (start us, length us, event | category | flops | bytes accessed | tf_op | source)
XLA Modules:
  0.0 178.6 jit_solution(12314584196743637060)
XLA Ops:
  3.8 3.4 %collective-permute-start.3 = (bf16[64,1024]{1,0:T(8,128)(2,1)S(1)}, bf16[64,1024]{1,0:T(8,128)(2,1)S(1)}, u32[]{:S(2)}, u32[]{:S(2)}) collective-permute-start(bf16[64,1024]{1,0:T(8,128)(2,1)S(1)} %copy-done.4), channel_id=1, source_target_pairs={{0,4},{1,5},{2,6},{3,7},{4,8},{5,9},{6,10},{7,11},{8,12},{9,13},{1... | collective-permute-start | bytes 393224 | tf_op jit(solution)/shard_map/ppermute | solution.py:455
  8.6 2.5 %first_weights.1 = (bf16[128,1024]{1,0:T(8,128)(2,1)}, bf16[128,1024]{1,0:T(8,128)(2,1)}, bf16[384,768]{1,0:T(8,128)(2,1)}) custom-call(bf16[3,64,1024]{2,1,0:T(8,128)(2,1)} %bitcast.20, bf16[64,1024]{1,0:T(8,128)(2,1)} %o_ref.1, bf16[7,96,100]{2,1,0:T(8,128)(2,1)} %pre_ref.1, bf16[144,768]{1,0:T(8,128)(2,1)} %bitcast.21, bf16[144,768]{1,0:T(8,128)(2,1)} %bitcast.22), custom_call_target="tpu_custom_call" | custom-call | bytes 3145728 | tf_op jit(solution)/shard_map/first_weights/pallas_call | solution.py:439
  12.7 6.4 %collective-permute-done.3.refs_4_ = bf16[64,1024]{1,0:T(8,128)(2,1)S(1)} collective-permute-done((bf16[64,1024]{1,0:T(8,128)(2,1)S(1)}, bf16[64,1024]{1,0:T(8,128)(2,1)S(1)}, u32[]{:S(2)}, u32[]{:S(2)}) %collective-permute-start.3) | collective-permute-done | bytes 131104 | tf_op jit(solution)/shard_map/ppermute | solution.py:455
  21.2 2.9 %collective-permute-done.2.refs_3_ = bf16[64,1024]{1,0:T(8,128)(2,1)S(1)} collective-permute-done((bf16[64,1024]{1,0:T(8,128)(2,1)S(1)}, bf16[64,1024]{1,0:T(8,128)(2,1)S(1)}, u32[]{:S(2)}, u32[]{:S(2)}) %collective-permute-start.2) | collective-permute-done | bytes 131104 | tf_op jit(solution)/shard_map/ppermute | solution.py:491
  26.3 4.9 %shard_map.141 = bf16[16,96,384]{2,1,0:T(8,128)(2,1)} custom-call(bf16[8,96,768]{2,1,0:T(8,128)(2,1)S(1)} %copy-done.1), custom_call_target="tpu_custom_call" | custom-call | bytes 3145728 | tf_op jit(solution)/shard_map/pallas_call | solution.py:43
  31.2 4.5 %all-to-all-start = ((bf16[16,96,384]{2,1,0:T(8,128)(2,1)}), bf16[16,96,384]{2,1,0:T(8,128)(2,1)}, u32[]{:S(2)}, u32[]{:S(2)}) async-start(bf16[16,96,384]{2,1,0:T(8,128)(2,1)} %shard_map.141), calls=%async_computation | async-start | bytes 2359296 | tf_op jit(solution)/shard_map/all_to_all | solution.py:390
  35.7 3.1 %collective-permute-start.28 = (bf16[384,768]{1,0:T(8,128)(2,1)}, bf16[384,768]{1,0:T(8,128)(2,1)S(1)}, u32[]{:S(2)}, u32[]{:S(2)}) collective-permute-start(bf16[384,768]{1,0:T(8,128)(2,1)} %get-tuple-element.35.own), channel_id=1, source_target_pairs={{0,12},{1,13},{2,14},{3,15},{4,0},{5,1},{6,2},{7,3},{8,4},{9,5},{1... | collective-permute-start | bytes 1769480 | tf_op jit(solution)/shard_map/ppermute | solution.py:464
  41.7 2.3 %collective-permute-start.5 = (bf16[64,1024]{1,0:T(8,128)(2,1)S(1)}, bf16[64,1024]{1,0:T(8,128)(2,1)S(1)}, u32[]{:S(2)}, u32[]{:S(2)}) collective-permute-start(bf16[64,1024]{1,0:T(8,128)(2,1)S(1)} %copy-done.18), channel_id=1, source_target_pairs={{0,2},{1,3},{2,0},{3,1},{4,6},{5,7},{6,4},{7,5},{8,10},{9,11},{10,... | collective-permute-start | bytes 393224 | tf_op jit(solution)/shard_map/ppermute | solution.py:492
  44.0 3.8 %collective-permute-done.5.refs_6_ = bf16[64,1024]{1,0:T(8,128)(2,1)S(1)} collective-permute-done((bf16[64,1024]{1,0:T(8,128)(2,1)S(1)}, bf16[64,1024]{1,0:T(8,128)(2,1)S(1)}, u32[]{:S(2)}, u32[]{:S(2)}) %collective-permute-start.5) | collective-permute-done | bytes 131104 | tf_op jit(solution)/shard_map/ppermute | solution.py:492
  48.6 4.8 %collective-permute-done.6.refs_7_ = bf16[64,1024]{1,0:T(8,128)(2,1)S(1)} collective-permute-done((bf16[64,1024]{1,0:T(8,128)(2,1)S(1)}, bf16[64,1024]{1,0:T(8,128)(2,1)S(1)}, u32[]{:S(2)}, u32[]{:S(2)}) %collective-permute-start.6) | collective-permute-done | bytes 131104 | tf_op jit(solution)/shard_map/ppermute | solution.py:492
  54.0 2.9 %collective-permute-start.12 = (bf16[128,1024]{1,0:T(8,128)(2,1)}, bf16[128,1024]{1,0:T(8,128)(2,1)}, u32[]{:S(2)}, u32[]{:S(2)}) collective-permute-start(bf16[128,1024]{1,0:T(8,128)(2,1)} %collective-permute-done.10.refs_13_), channel_id=1, source_target_pairs={{0,12},{1,13},{2,14},{3,15},{4,0},{5,1},{6,2},{7,3},{8,4},{9,5},{1... | collective-permute-start | bytes 786440 | tf_op jit(solution)/shard_map/ppermute | solution.py:461
  57.6 7.0 %collective-permute-done.28.right = bf16[384,768]{1,0:T(8,128)(2,1)S(1)} collective-permute-done((bf16[384,768]{1,0:T(8,128)(2,1)}, bf16[384,768]{1,0:T(8,128)(2,1)S(1)}, u32[]{:S(2)}, u32[]{:S(2)}) %collective-permute-start.28) | collective-permute-done | bytes 589856 | tf_op jit(solution)/shard_map/ppermute | solution.py:464
  70.3 8.9 %attention.1 = (bf16[64,1024]{1,0:T(8,128)(2,1)}, bf16[64,1024]{1,0:T(8,128)(2,1)}, bf16[64,1024]{1,0:T(8,128)(2,1)}, bf16[64,1024]{1,0:T(8,128)(2,1)}) custom-call(s32[1]{0:T(128)} %bitcast.flag_ref, f32[8,1024]{1,0:T(8,128)} %mod_ref.5, bf16[64,1024]{1,0:T(8,128)(2,1)} %frames_ref.1, bf16[64,1024]{1,0:T(8,128)(2,1)} %copy-done.19, ...), custom_call_target="tpu_custom_call" | custom-call | flops 1000000000 | bytes 4194304 | tf_op jit(solution)/shard_map/attention/pallas_call | solution.py:507
  79.4 2.5 %collective-permute-start.14 = (bf16[64,1024]{1,0:T(8,128)(2,1)}, bf16[64,1024]{1,0:T(8,128)(2,1)S(1)}, u32[]{:S(2)}, u32[]{:S(2)}) collective-permute-start(bf16[64,1024]{1,0:T(8,128)(2,1)} %get-tuple-element.26), channel_id=1, source_target_pairs={{0,2},{1,3},{2,0},{3,1},{4,6},{5,7},{6,4},{7,5},{8,10},{9,11},{10,... | collective-permute-start | bytes 393224 | tf_op jit(solution)/shard_map/ppermute | solution.py:540
  81.9 3.2 %voc_merge.1 = (bf16[4,96,768]{2,1,0:T(8,128)(2,1)}, bf16[4,144,768]{2,1,0:T(8,128)(2,1)}, bf16[4,144,768]{2,1,0:T(8,128)(2,1)}) custom-call(bf16[384,768]{1,0:T(8,128)(2,1)} %get-tuple-element.35.own, bf16[384,768]{1,0:T(8,128)(2,1)} %copy-done.9, bf16[384,768]{1,0:T(8,128)(2,1)} %copy-done.10, bf16[240,768]{1,0:T(8,128)(2,1)} %collective-permute-done.29.far_top, ...), custom_call_target="tpu_custom_call" | custom-call | bytes 5242880 | tf_op jit(solution)/shard_map/voc_merge/pallas_call | solution.py:469
  88.9 2.9 %collective-permute-start.16 = (bf16[64,1024]{1,0:T(8,128)(2,1)S(1)}, bf16[64,1024]{1,0:T(8,128)(2,1)S(1)}, u32[]{:S(2)}, u32[]{:S(2)}) collective-permute-start(bf16[64,1024]{1,0:T(8,128)(2,1)S(1)} %get-tuple-element.29.h0), channel_id=1, source_target_pairs={{0,8},{1,9},{2,10},{3,11},{4,12},{5,13},{6,14},{7,15},{8,0},{9,1},... | collective-permute-start | bytes 393224 | tf_op jit(solution)/shard_map/ppermute | solution.py:552
  91.8 3.2 %collective-permute-start.18 = (bf16[64,1024]{1,0:T(8,128)(2,1)S(1)}, bf16[64,1024]{1,0:T(8,128)(2,1)S(1)}, u32[]{:S(2)}, u32[]{:S(2)}) collective-permute-start(bf16[64,1024]{1,0:T(8,128)(2,1)S(1)} %get-tuple-element.29.h0), channel_id=1, source_target_pairs={{0,12},{1,13},{2,14},{3,15},{4,0},{5,1},{6,2},{7,3},{8,4},{9,5},{1... | collective-permute-start | bytes 393224 | tf_op jit(solution)/shard_map/ppermute | solution.py:554
  100.6 3.1 %shard_map.143 = (bf16[64,1024]{1,0:T(8,128)(2,1)S(1)}, bf16[64,1024]{1,0:T(8,128)(2,1)S(1)}, bf16[64,1024]{1,0:T(8,128)(2,1)S(1)}, bf16[64,1024]{1,0:T(8,128)(2,1)S(1)}) custom-call(bf16[64,1024]{1,0:T(8,128)(2,1)S(1)} %get-tuple-element.29.h0, bf16[64,1024]{1,0:T(8,128)(2,1)S(1)} %collective-permute-done.16.h1, ...), custom_call_target="tpu_custom_call" | custom-call | flops 1100000000 | bytes 5242880 | tf_op jit(solution)/shard_map/pallas_call | solution.py:43
  105.5 2.3 %collective-permute-start.23 = (bf16[64,1024]{1,0:T(8,128)(2,1)S(1)}, bf16[64,1024]{1,0:T(8,128)(2,1)S(1)}, u32[]{:S(2)}, u32[]{:S(2)}) collective-permute-start(bf16[64,1024]{1,0:T(8,128)(2,1)S(1)} %get-tuple-element.32), channel_id=1, source_target_pairs={{0,12},{1,13},{2,14},{3,15},{4,0},{5,1},{6,2},{7,3},{8,4},{9,5},{1... | collective-permute-start | bytes 393224 | tf_op jit(solution)/shard_map/ppermute | solution.py:566
  107.8 2.4 %collective-permute-done.22.p1 = bf16[64,1024]{1,0:T(8,128)(2,1)S(1)} collective-permute-done((bf16[64,1024]{1,0:T(8,128)(2,1)S(1)}, bf16[64,1024]{1,0:T(8,128)(2,1)S(1)}, u32[]{:S(2)}, u32[]{:S(2)}) %collective-permute-start.22) | collective-permute-done | bytes 131104 | tf_op jit(solution)/shard_map/ppermute | solution.py:565
  110.2 2.6 %collective-permute-start.24 = (bf16[64,1024]{1,0:T(8,128)(2,1)S(1)}, bf16[64,1024]{1,0:T(8,128)(2,1)S(1)}, u32[]{:S(2)}, u32[]{:S(2)}) collective-permute-start(bf16[64,1024]{1,0:T(8,128)(2,1)S(1)} %get-tuple-element.33), channel_id=1, source_target_pairs={{0,4},{1,5},{2,6},{3,7},{4,8},{5,9},{6,10},{7,11},{8,12},{9,13},{1... | collective-permute-start | bytes 393224 | tf_op jit(solution)/shard_map/ppermute | solution.py:567
  113.2 3.2 %collective-permute-done.24.p3 = bf16[64,1024]{1,0:T(8,128)(2,1)S(1)} collective-permute-done((bf16[64,1024]{1,0:T(8,128)(2,1)S(1)}, bf16[64,1024]{1,0:T(8,128)(2,1)S(1)}, u32[]{:S(2)}, u32[]{:S(2)}) %collective-permute-start.24) | collective-permute-done | bytes 131104 | tf_op jit(solution)/shard_map/ppermute | solution.py:567
  117.6 3.6 %all-to-all-start.1 = ((f32[16,64,100]{2,1,0:T(8,128)}), f32[16,64,100]{2,1,0:T(8,128)S(1)}, u32[]{:S(2)}, u32[]{:S(2)}) async-start(f32[16,64,100]{2,1,0:T(8,128)} %shard_map.144), calls=%async_computation.1 | async-start | bytes 1048576 | tf_op jit(solution)/shard_map/all_to_all | solution.py:390
  122.6 9.4 %all-to-all-done.1.mel_ref = f32[16,64,100]{2,1,0:T(8,128)S(1)} async-done(((f32[16,64,100]{2,1,0:T(8,128)}), f32[16,64,100]{2,1,0:T(8,128)S(1)}, u32[]{:S(2)}, u32[]{:S(2)}) %all-to-all-start.1) | async-done | bytes 409632 | tf_op jit(solution)/shard_map/all_to_all | solution.py:390
  134.7 3.9 %prelude_weights.1 = bf16[16,96,768]{2,1,0:T(8,128)(2,1)} custom-call(s32[2]{0:T(128)} %pad_add_fusion.place_ref, bf16[4,96,768]{2,1,0:T(8,128)(2,1)} %get-tuple-element.36.p0, bf16[4,96,768]{2,1,0:T(8,128)(2,1)} %copy-done.13, bf16[4,96,768]{2,1,0:T(8,128)(2,1)} %collective-permute-done.32.p2, bf16[4,96,768]{2,1,0:T(8,128)(2,1)} %collective-permute-done.33.p3), custom_call_target="tpu_custom_call" | custom-call | bytes 5242880 | tf_op jit(solution)/shard_map/prelude_weights/pallas_call | solution.py:579
  138.6 3.2 %collective-permute-done.25.before_ref = f32[8,100]{1,0:T(8,128)S(1)} collective-permute-done((f32[8,100]{1,0:T(8,128)S(1)}, f32[8,100]{1,0:T(8,128)S(1)}, u32[]{:S(2)}, u32[]{:S(2)}) %collective-permute-start.25) | collective-permute-done | bytes 3232 | tf_op jit(solution)/shard_map/ppermute | solution.py:599
  141.8 4.3 %collective-permute-start.26 = (f32[8,100]{1,0:T(8,128)S(1)}, f32[8,100]{1,0:T(8,128)S(1)}, u32[]{:S(2)}, u32[]{:S(2)}) collective-permute-start(f32[8,100]{1,0:T(8,128)S(1)} %get-tuple-element.44), channel_id=1, source_target_pairs={{16,0},{32,16},{48,32},{64,48},{80,64},{96,80},{112,96},{128,112},... | collective-permute-start | bytes 9608 | tf_op jit(solution)/shard_map/ppermute | solution.py:600
  146.2 3.4 %convolution_bitcast_fusion.comp_ref = f32[768,384]{1,0:T(8,128)S(1)} fusion(bf16[16,96,768]{2,1,0:T(8,128)(2,1)} %prelude_weights.1, bf16[16,96,384]{2,1,0:T(8,128)(2,1)} %all-to-all-done), kind=kOutput, calls=%fused_computation | convolution fusion | flops 905969664 | bytes 4718592 | tf_op jit(solution)/shard_map/dot_general | solution.py:589
  149.9 2.5 %shard_map.146 = bf16[16,72,192]{2,1,0:T(8,128)(2,1)} custom-call(s32[2]{0:T(128)S(1)} %add_convert_fusion.1.flag_ref, f32[16,64,100]{2,1,0:T(8,128)S(1)} %all-to-all-done.1.mel_ref, f32[8,100]{1,0:T(8,128)S(1)} %collective-permute-done.25.before_ref, f32[8,100]{1,0:T(8,128)S(1)} %collective-permute-done.26.after_ref, ...), custom_call_target="tpu_custom_call" | custom-call | flops 500000000 | bytes 2097152 | tf_op jit(solution)/shard_map/pallas_call | solution.py:43
  152.4 3.6 %all-to-all-start.2 = ((bf16[16,72,192]{2,1,0:T(8,128)(2,1)}), bf16[16,72,192]{2,1,0:T(8,128)(2,1)S(1)}, u32[]{:S(2)}, u32[]{:S(2)}) async-start(bf16[16,72,192]{2,1,0:T(8,128)(2,1)} %shard_map.146), calls=%async_computation.2 | async-start | bytes 1179648 | tf_op jit(solution)/shard_map/all_to_all | solution.py:390
  157.6 9.8 %all-to-all-done.2.up_ref = bf16[16,72,192]{2,1,0:T(8,128)(2,1)S(1)} async-done(((bf16[16,72,192]{2,1,0:T(8,128)(2,1)}), bf16[16,72,192]{2,1,0:T(8,128)(2,1)S(1)}, u32[]{:S(2)}, u32[]{:S(2)}) %all-to-all-start.2) | async-done | bytes 442400 | tf_op jit(solution)/shard_map/all_to_all | solution.py:390
  168.3 8.3 %convolutions.1 = bf16[64,3072]{1,0:T(8,128)(2,1)} custom-call(s32[2]{0:T(128)} %add_convert_fusion.flag_ref, s32[2]{0:T(128)} %pad_add_fusion.place_ref, bf16[16,72,192]{2,1,0:T(8,128)(2,1)} %copy-done.8, f32[2,768]{1,0:T(2,128)} %alpha_ref.1, bf16[4,144,768]{2,1,0:T(8,128)(2,1)} %get-tuple-element.40.refs_0_, bf16[4,144,768]{2,1,0:T(8,128)(2,1)} %copy-done.12, ...), custom_call_target="tpu_custom_call" | custom-call | flops 2000000000 | bytes 8388608 | tf_op jit(solution)/shard_map/convolutions/pallas_call | solution.py:619
  (128 shorter events, 42.7 us)
Async XLA Ops:
  2.9 36.4 %collective-permute-start.20 = (bf16[2048,256]{1,0:T(8,128)(2,1)S(1)}, bf16[2048,256]{1,0:T(8,128)(2,1)}, u32[]{:S(2)}, u32[]{:S(2)}) collective-permute-start(bf16[2048,256]{1,0:T(8,128)(2,1)S(1)} %shard_map.142.w0), channel_id=1, source_target_pairs={{0,130},{1,131},{2,128},{3,129},{4,134},{5,135},{6,132},{7,133},{8... | collective-permute-start | bytes 3145736 | tf_op jit(solution)/shard_map/ppermute | solution.py:498
  3.8 15.3 %collective-permute-start.3 = (bf16[64,1024]{1,0:T(8,128)(2,1)S(1)}, bf16[64,1024]{1,0:T(8,128)(2,1)S(1)}, u32[]{:S(2)}, u32[]{:S(2)}) collective-permute-start(bf16[64,1024]{1,0:T(8,128)(2,1)S(1)} %copy-done.4), channel_id=1, source_target_pairs={{0,4},{1,5},{2,6},{3,7},{4,8},{5,9},{6,10},{7,11},{8,12},{9,13},{1... | collective-permute-start | bytes 393224 | tf_op jit(solution)/shard_map/ppermute | solution.py:455
  7.2 12.0 %collective-permute-start = (bf16[64,1024]{1,0:T(8,128)(2,1)S(1)}, bf16[64,1024]{1,0:T(8,128)(2,1)S(1)}, u32[]{:S(2)}, u32[]{:S(2)}) collective-permute-start(bf16[64,1024]{1,0:T(8,128)(2,1)S(1)} %copy-done.4), channel_id=1, source_target_pairs={{0,1},{1,0},{2,3},{3,2},{4,5},{5,4},{6,7},{7,6},{8,9},{9,8},{10,11... | collective-permute-start | bytes 393224 | tf_op jit(solution)/shard_map/ppermute | solution.py:491
  7.3 12.0 %collective-permute-start.1 = (bf16[64,1024]{1,0:T(8,128)(2,1)S(1)}, bf16[64,1024]{1,0:T(8,128)(2,1)S(1)}, u32[]{:S(2)}, u32[]{:S(2)}) collective-permute-start(bf16[64,1024]{1,0:T(8,128)(2,1)S(1)} %copy-done.4), channel_id=1, source_target_pairs={{0,2},{1,3},{2,0},{3,1},{4,6},{5,7},{6,4},{7,5},{8,10},{9,11},{10,... | collective-permute-start | bytes 393224 | tf_op jit(solution)/shard_map/ppermute | solution.py:491
  11.2 13.0 %collective-permute-start.7 = (bf16[128,1024]{1,0:T(8,128)(2,1)}, bf16[128,1024]{1,0:T(8,128)(2,1)S(1)}, u32[]{:S(2)}, u32[]{:S(2)}) collective-permute-start(bf16[128,1024]{1,0:T(8,128)(2,1)} %get-tuple-element.22.refs_8_), channel_id=1, source_target_pairs={{0,4},{1,5},{2,6},{3,7},{4,8},{5,9},{6,10},{7,11},{8,12},{9,13},{1... | collective-permute-start | bytes 786440 | tf_op jit(solution)/shard_map/ppermute | solution.py:456
  19.1 16.6 %collective-permute-start.10 = (bf16[128,1024]{1,0:T(8,128)(2,1)}, bf16[128,1024]{1,0:T(8,128)(2,1)}, u32[]{:S(2)}, u32[]{:S(2)}) collective-permute-start(bf16[128,1024]{1,0:T(8,128)(2,1)} %get-tuple-element.23.refs_9_), channel_id=1, source_target_pairs={{0,12},{1,13},{2,14},{3,15},{4,0},{5,1},{6,2},{7,3},{8,4},{9,5},{1... | collective-permute-start | bytes 786440 | tf_op jit(solution)/shard_map/ppermute | solution.py:457
  19.2 19.6 %collective-permute-start.8 = (bf16[128,1024]{1,0:T(8,128)(2,1)}, bf16[128,1024]{1,0:T(8,128)(2,1)}, u32[]{:S(2)}, u32[]{:S(2)}) collective-permute-start(bf16[128,1024]{1,0:T(8,128)(2,1)} %get-tuple-element.23.refs_9_), channel_id=1, source_target_pairs={{0,4},{1,5},{2,6},{3,7},{4,8},{5,9},{6,10},{7,11},{8,12},{9,13},{1... | collective-permute-start | bytes 786440 | tf_op jit(solution)/shard_map/ppermute | solution.py:458
  24.2 14.7 %collective-permute-start.9 = (bf16[128,1024]{1,0:T(8,128)(2,1)}, bf16[128,1024]{1,0:T(8,128)(2,1)}, u32[]{:S(2)}, u32[]{:S(2)}) collective-permute-start(bf16[128,1024]{1,0:T(8,128)(2,1)} %get-tuple-element.22.refs_8_), channel_id=1, source_target_pairs={{0,12},{1,13},{2,14},{3,15},{4,0},{5,1},{6,2},{7,3},{8,4},{9,5},{1... | collective-permute-start | bytes 786440 | tf_op jit(solution)/shard_map/ppermute | solution.py:459
  24.8 28.5 %collective-permute-start.27 = (bf16[384,768]{1,0:T(8,128)(2,1)}, bf16[384,768]{1,0:T(8,128)(2,1)S(1)}, u32[]{:S(2)}, u32[]{:S(2)}) collective-permute-start(bf16[384,768]{1,0:T(8,128)(2,1)} %get-tuple-element.35.own), channel_id=1, source_target_pairs={{0,4},{1,5},{2,6},{3,7},{4,8},{5,9},{6,10},{7,11},{8,12},{9,13},{1... | collective-permute-start | bytes 1769480 | tf_op jit(solution)/shard_map/ppermute | solution.py:463
  31.2 57.7 %all-to-all-start = ((bf16[16,96,384]{2,1,0:T(8,128)(2,1)}), bf16[16,96,384]{2,1,0:T(8,128)(2,1)}, u32[]{:S(2)}, u32[]{:S(2)}) async-start(bf16[16,96,384]{2,1,0:T(8,128)(2,1)} %shard_map.141), calls=%async_computation | async-start | bytes 2359296 | tf_op jit(solution)/shard_map/all_to_all | solution.py:390
  35.7 28.9 %collective-permute-start.28 = (bf16[384,768]{1,0:T(8,128)(2,1)}, bf16[384,768]{1,0:T(8,128)(2,1)S(1)}, u32[]{:S(2)}, u32[]{:S(2)}) collective-permute-start(bf16[384,768]{1,0:T(8,128)(2,1)} %get-tuple-element.35.own), channel_id=1, source_target_pairs={{0,12},{1,13},{2,14},{3,15},{4,0},{5,1},{6,2},{7,3},{8,4},{9,5},{1... | collective-permute-start | bytes 1769480 | tf_op jit(solution)/shard_map/ppermute | solution.py:464
  38.9 52.9 %collective-permute-start.19 = (bf16[2048,256]{1,0:T(8,128)(2,1)S(1)}, bf16[2048,256]{1,0:T(8,128)(2,1)S(1)}, u32[]{:S(2)}, u32[]{:S(2)}) collective-permute-start(bf16[2048,256]{1,0:T(8,128)(2,1)S(1)} %shard_map.142.w0), channel_id=1, source_target_pairs={{0,1},{1,0},{2,3},{3,2},{4,5},{5,4},{6,7},{7,6},{8,9},{9,8},{10,11... | collective-permute-start | bytes 3145736 | tf_op jit(solution)/shard_map/ppermute | solution.py:497
  39.4 61.2 %collective-permute-start.21 = (bf16[2048,256]{1,0:T(8,128)(2,1)}, bf16[2048,256]{1,0:T(8,128)(2,1)}, u32[]{:S(2)}, u32[]{:S(2)}) collective-permute-start(bf16[2048,256]{1,0:T(8,128)(2,1)} %collective-permute-done.20.w2), channel_id=1, source_target_pairs={{0,1},{1,0},{2,3},{3,2},{4,5},{5,4},{6,7},{7,6},{8,9},{9,8},{10,11... | collective-permute-start | bytes 3145736 | tf_op jit(solution)/shard_map/ppermute | solution.py:499
  53.3 13.4 %collective-permute-start.11 = (bf16[128,1024]{1,0:T(8,128)(2,1)S(1)}, bf16[128,1024]{1,0:T(8,128)(2,1)S(1)}, u32[]{:S(2)}, u32[]{:S(2)}) collective-permute-start(bf16[128,1024]{1,0:T(8,128)(2,1)S(1)} %collective-permute-done.7.refs_10_), channel_id=1, source_target_pairs={{0,4},{1,5},{2,6},{3,7},{4,8},{5,9},{6,10},{7,11},{8,12},{9,13},{1... | collective-permute-start | bytes 786440 | tf_op jit(solution)/shard_map/ppermute | solution.py:460
  54.0 16.4 %collective-permute-start.12 = (bf16[128,1024]{1,0:T(8,128)(2,1)}, bf16[128,1024]{1,0:T(8,128)(2,1)}, u32[]{:S(2)}, u32[]{:S(2)}) collective-permute-start(bf16[128,1024]{1,0:T(8,128)(2,1)} %collective-permute-done.10.refs_13_), channel_id=1, source_target_pairs={{0,12},{1,13},{2,14},{3,15},{4,0},{5,1},{6,2},{7,3},{8,4},{9,5},{1... | collective-permute-start | bytes 786440 | tf_op jit(solution)/shard_map/ppermute | solution.py:461
  64.6 17.2 %collective-permute-start.29 = (bf16[240,768]{1,0:T(8,128)(2,1)}, bf16[240,768]{1,0:T(8,128)(2,1)}, u32[]{:S(2)}, u32[]{:S(2)}) collective-permute-start(bf16[240,768]{1,0:T(8,128)(2,1)} %slice.18), channel_id=1, source_target_pairs={{0,4},{1,5},{2,6},{3,7},{4,8},{5,9},{6,10},{7,11},{8,12},{9,13},{1... | collective-permute-start | bytes 1105928 | tf_op jit(solution)/shard_map/ppermute | solution.py:465
  67.4 11.9 %collective-permute-start.30 = (bf16[144,768]{1,0:T(8,128)(2,1)}, bf16[144,768]{1,0:T(8,128)(2,1)}, u32[]{:S(2)}, u32[]{:S(2)}) collective-permute-start(bf16[144,768]{1,0:T(8,128)(2,1)} %slice.19), channel_id=1, source_target_pairs={{0,12},{1,13},{2,14},{3,15},{4,0},{5,1},{6,2},{7,3},{8,4},{9,5},{1... | collective-permute-start | bytes 663560 | tf_op jit(solution)/shard_map/ppermute | solution.py:466
  85.2 36.3 %collective-permute-start.32 = (bf16[4,96,768]{2,1,0:T(8,128)(2,1)}, bf16[4,96,768]{2,1,0:T(8,128)(2,1)}, u32[]{:S(2)}, u32[]{:S(2)}) collective-permute-start(bf16[4,96,768]{2,1,0:T(8,128)(2,1)} %get-tuple-element.36.p0), channel_id=1, source_target_pairs={{0,130},{1,131},{2,128},{3,129},{4,134},{5,135},{6,132},{7,133},{8... | collective-permute-start | bytes 1769480 | tf_op jit(solution)/shard_map/ppermute | solution.py:480
  88.9 8.0 %collective-permute-start.16 = (bf16[64,1024]{1,0:T(8,128)(2,1)S(1)}, bf16[64,1024]{1,0:T(8,128)(2,1)S(1)}, u32[]{:S(2)}, u32[]{:S(2)}) collective-permute-start(bf16[64,1024]{1,0:T(8,128)(2,1)S(1)} %get-tuple-element.29.h0), channel_id=1, source_target_pairs={{0,8},{1,9},{2,10},{3,11},{4,12},{5,13},{6,14},{7,15},{8,0},{9,1},... | collective-permute-start | bytes 393224 | tf_op jit(solution)/shard_map/ppermute | solution.py:552
  91.8 8.8 %collective-permute-start.18 = (bf16[64,1024]{1,0:T(8,128)(2,1)S(1)}, bf16[64,1024]{1,0:T(8,128)(2,1)S(1)}, u32[]{:S(2)}, u32[]{:S(2)}) collective-permute-start(bf16[64,1024]{1,0:T(8,128)(2,1)S(1)} %get-tuple-element.29.h0), channel_id=1, source_target_pairs={{0,12},{1,13},{2,14},{3,15},{4,0},{5,1},{6,2},{7,3},{8,4},{9,5},{1... | collective-permute-start | bytes 393224 | tf_op jit(solution)/shard_map/ppermute | solution.py:554
  96.8 35.3 %collective-permute-start.35 = (bf16[4,144,768]{2,1,0:T(8,128)(2,1)}, bf16[4,144,768]{2,1,0:T(8,128)(2,1)}, u32[]{:S(2)}, u32[]{:S(2)}) collective-permute-start(bf16[4,144,768]{2,1,0:T(8,128)(2,1)} %get-tuple-element.40.refs_0_), channel_id=1, source_target_pairs={{0,130},{1,131},{2,128},{3,129},{4,134},{5,135},{6,132},{7,133},{8... | collective-permute-start | bytes 2654216 | tf_op jit(solution)/shard_map/ppermute | solution.py:481
  98.9 33.7 %collective-permute-start.38 = (bf16[4,144,768]{2,1,0:T(8,128)(2,1)}, bf16[4,144,768]{2,1,0:T(8,128)(2,1)}, u32[]{:S(2)}, u32[]{:S(2)}) collective-permute-start(bf16[4,144,768]{2,1,0:T(8,128)(2,1)} %get-tuple-element.41.refs_4_), channel_id=1, source_target_pairs={{0,2},{1,3},{2,0},{3,1},{4,6},{5,7},{6,4},{7,5},{8,10},{9,11},{10,... | collective-permute-start | bytes 2654216 | tf_op jit(solution)/shard_map/ppermute | solution.py:482
  117.6 14.4 %all-to-all-start.1 = ((f32[16,64,100]{2,1,0:T(8,128)}), f32[16,64,100]{2,1,0:T(8,128)S(1)}, u32[]{:S(2)}, u32[]{:S(2)}) async-start(f32[16,64,100]{2,1,0:T(8,128)} %shard_map.144), calls=%async_computation.1 | async-start | bytes 1048576 | tf_op jit(solution)/shard_map/all_to_all | solution.py:390
  121.2 10.8 %collective-permute-start.31 = (bf16[4,96,768]{2,1,0:T(8,128)(2,1)}, bf16[4,96,768]{2,1,0:T(8,128)(2,1)S(1)}, u32[]{:S(2)}, u32[]{:S(2)}) collective-permute-start(bf16[4,96,768]{2,1,0:T(8,128)(2,1)} %get-tuple-element.36.p0), channel_id=1, source_target_pairs={{0,1},{1,0},{2,3},{3,2},{4,5},{5,4},{6,7},{7,6},{8,9},{9,8},{10,11... | collective-permute-start | bytes 1769480 | tf_op jit(solution)/shard_map/ppermute | solution.py:483
  121.5 11.2 %collective-permute-start.33 = (bf16[4,96,768]{2,1,0:T(8,128)(2,1)}, bf16[4,96,768]{2,1,0:T(8,128)(2,1)}, u32[]{:S(2)}, u32[]{:S(2)}) collective-permute-start(bf16[4,96,768]{2,1,0:T(8,128)(2,1)} %collective-permute-done.32.p2), channel_id=1, source_target_pairs={{0,1},{1,0},{2,3},{3,2},{4,5},{5,4},{6,7},{7,6},{8,9},{9,8},{10,11... | collective-permute-start | bytes 1769480 | tf_op jit(solution)/shard_map/ppermute | solution.py:486
  122.4 35.2 %collective-permute-start.34 = (bf16[4,144,768]{2,1,0:T(8,128)(2,1)S(1)}, bf16[4,144,768]{2,1,0:T(8,128)(2,1)S(1)}, u32[]{:S(2)}, u32[]{:S(2)}) collective-permute-start(bf16[4,144,768]{2,1,0:T(8,128)(2,1)S(1)} %copy-done.11), channel_id=1, source_target_pairs={{0,1},{1,0},{2,3},{3,2},{4,5},{5,4},{6,7},{7,6},{8,9},{9,8},{10,11... | collective-permute-start | bytes 2654216 | tf_op jit(solution)/shard_map/ppermute | solution.py:484
  132.0 25.6 %collective-permute-start.37 = (bf16[4,144,768]{2,1,0:T(8,128)(2,1)}, bf16[4,144,768]{2,1,0:T(8,128)(2,1)}, u32[]{:S(2)}, u32[]{:S(2)}) collective-permute-start(bf16[4,144,768]{2,1,0:T(8,128)(2,1)} %get-tuple-element.41.refs_4_), channel_id=1, source_target_pairs={{0,1},{1,0},{2,3},{3,2},{4,5},{5,4},{6,7},{7,6},{8,9},{9,8},{10,11... | collective-permute-start | bytes 2654216 | tf_op jit(solution)/shard_map/ppermute | solution.py:485
  132.1 25.5 %collective-permute-start.36 = (bf16[4,144,768]{2,1,0:T(8,128)(2,1)}, bf16[4,144,768]{2,1,0:T(8,128)(2,1)}, u32[]{:S(2)}, u32[]{:S(2)}) collective-permute-start(bf16[4,144,768]{2,1,0:T(8,128)(2,1)} %collective-permute-done.35.refs_2_), channel_id=1, source_target_pairs={{0,1},{1,0},{2,3},{3,2},{4,5},{5,4},{6,7},{7,6},{8,9},{9,8},{10,11... | collective-permute-start | bytes 2654216 | tf_op jit(solution)/shard_map/ppermute | solution.py:487
  132.6 25.0 %collective-permute-start.39 = (bf16[4,144,768]{2,1,0:T(8,128)(2,1)}, bf16[4,144,768]{2,1,0:T(8,128)(2,1)}, u32[]{:S(2)}, u32[]{:S(2)}) collective-permute-start(bf16[4,144,768]{2,1,0:T(8,128)(2,1)} %collective-permute-done.38.refs_6_), channel_id=1, source_target_pairs={{0,1},{1,0},{2,3},{3,2},{4,5},{5,4},{6,7},{7,6},{8,9},{9,8},{10,11... | collective-permute-start | bytes 2654216 | tf_op jit(solution)/shard_map/ppermute | solution.py:488
  132.7 9.1 %collective-permute-start.25 = (f32[8,100]{1,0:T(8,128)S(1)}, f32[8,100]{1,0:T(8,128)S(1)}, u32[]{:S(2)}, u32[]{:S(2)}) collective-permute-start(f32[8,100]{1,0:T(8,128)S(1)} %get-tuple-element.45), channel_id=1, source_target_pairs={{0,16},{16,32},{32,48},{48,64},{64,80},{80,96},{96,112},{112,128},... | collective-permute-start | bytes 9608 | tf_op jit(solution)/shard_map/ppermute | solution.py:599
  141.8 8.1 %collective-permute-start.26 = (f32[8,100]{1,0:T(8,128)S(1)}, f32[8,100]{1,0:T(8,128)S(1)}, u32[]{:S(2)}, u32[]{:S(2)}) collective-permute-start(f32[8,100]{1,0:T(8,128)S(1)} %get-tuple-element.44), channel_id=1, source_target_pairs={{16,0},{32,16},{48,32},{64,48},{80,64},{96,80},{112,96},{128,112},... | collective-permute-start | bytes 9608 | tf_op jit(solution)/shard_map/ppermute | solution.py:600
  152.4 15.1 %all-to-all-start.2 = ((bf16[16,72,192]{2,1,0:T(8,128)(2,1)}), bf16[16,72,192]{2,1,0:T(8,128)(2,1)S(1)}, u32[]{:S(2)}, u32[]{:S(2)}) async-start(bf16[16,72,192]{2,1,0:T(8,128)(2,1)} %shard_map.146), calls=%async_computation.2 | async-start | bytes 1179648 | tf_op jit(solution)/shard_map/all_to_all | solution.py:390
  (36 other events, 363.6 us)
where the time goes:
time: 179 us
  waiting for transfers between devices  62.1 us (35%)
  starting transfers between devices  61.4 us (34%)
  Pallas kernels  39.2 us (22%)
  local copies, waits for them, and re-layouts  10.1 us (6%)
  matrix products  3.38 us (2%)
    all_to_all x3, waiting for transfers between devices, exchange(): lax.all_to_all(value, axis, 0, 0, tiled=True, axis_index_groups=groups)  19.2 us
    pallas_call x7, Pallas kernels, whole(): pl.pallas_call(kernel, out_shape=out_shapes, in_specs=[pl.BlockSpec(memor...  12.4 us
    all_to_all x3, starting transfers between devices, exchange(): lax.all_to_all(value, axis, 0, 0, tiled=True, axis_index_groups=groups)  11.7 us
    ppermute x3, waiting for transfers between devices, program(): lax.ppermute(back_frames, 'sub', beside[k - 1])  10.8 us
    pallas_call x1, Pallas kernels, program(): pl.pallas_call(attention_kernel, out_shape=(quarter,) * 4, in_specs=[pl.B...  8.89 us
    pallas_call x1, Pallas kernels, program(): pl.pallas_call(conv_kernel, out_shape=shape((64, 3072), bf16), in_specs=[...  8.29 us
    ppermute x1, waiting for transfers between devices, program(): voc_right = lax.ppermute(w_voc, 'sub', to_left)  6.99 us
    unnamed x53, local copies, waits for them, and re-layouts  6.56 us
  transfers between devices with their start and end apart: 43, of which 16 were waited for; matrix products, arithmetic and copies ran while one was open for 4% of the time, Pallas kernels for 17%

commit v1 on v0

--- a/solution.py
+++ b/solution.py
@@ -88,15 +88,9 @@
 
 
 def upsample_weights_kernel(w_ref, out_ref):
-    def half(g, carry):
-        lanes = pl.ds(pl.multiple_of(384 * g, 384), 384)
+    for s in range(16):
         for t, tap in enumerate(TAP_ORDER):
-            rows = w_ref[tap, :, lanes]
-            for i in range(8):
-                out_ref[8 * g + i, :, 48 * t : 48 * t + 48] = rows[:, 48 * i : 48 * i + 48]
-        return carry
-
-    lax.fori_loop(0, 2, half, 0)
+            out_ref[s, :, 48 * t : 48 * t + 48] = w_ref[tap, :, 48 * s : 48 * s + 48]
 
 
 def attention_kernel(flag_ref, mod_ref, *refs):

time: 179 us -> 177 us (0.989)
  Pallas kernels: 39.2 us -> 36.8 us
    pallas_call x7, Pallas kernels: 12.4 us -> 9.96 us  [whole(): pl.pallas_call(kernel, out_shape=out_shapes, in_specs=[pl.BlockSpec(memor...]
  transfers between devices with their start and end apart: 43 -> 43, of which waited for: 16 -> 16; matrix products, arithmetic and copies ran while one was open for 4% -> 4% of each run, Pallas kernels for 17% -> 16%
where the time goes in v1:
time: 177 us; the launch traced here: 176 us
  waiting for transfers between devices  62.4 us (35%)
  starting transfers between devices  61.1 us (35%)
  Pallas kernels  36.8 us (21%)
  local copies, waits for them, and re-layouts  10.1 us (6%)
  matrix products  3.39 us (2%)
    all_to_all x3, waiting for transfers between devices, exchange(): lax.all_to_all(value, axis, 0, 0, tiled=True, axis_index_groups=groups)  19.2 us
    all_to_all x3, starting transfers between devices, exchange(): lax.all_to_all(value, axis, 0, 0, tiled=True, axis_index_groups=groups)  11.7 us
    ppermute x3, waiting for transfers between devices, program(): lax.ppermute(back_frames, 'sub', beside[k - 1])  10.8 us
    pallas_call x7, Pallas kernels, whole(): pl.pallas_call(kernel, out_shape=out_shapes, in_specs=[pl.BlockSpec(memor...  9.96 us
    pallas_call x1, Pallas kernels, program(): pl.pallas_call(attention_kernel, out_shape=(quarter,) * 4, in_specs=[pl.B...  8.9 us
    pallas_call x1, Pallas kernels, program(): pl.pallas_call(conv_kernel, out_shape=shape((64, 3072), bf16), in_specs=[...  8.3 us
    ppermute x1, waiting for transfers between devices, program(): voc_right = lax.ppermute(w_voc, 'sub', to_left)  6.99 us
    unnamed x53, local copies, waits for them, and re-layouts  6.56 us
  transfers between devices with their start and end apart: 43, of which 16 were waited for; matrix products, arithmetic and copies ran while one was open for 4% of the time, Pallas kernels for 16%

profile of v1, /device:TPU:16, one launch (start us, length us, event | category | flops | bytes accessed | tf_op | source)
XLA Modules:
  0.0 176.2 jit_solution(77517242333215632)
XLA Ops:
  3.8 3.4 %collective-permute-start.3 = (bf16[64,1024]{1,0:T(8,128)(2,1)S(1)}, bf16[64,1024]{1,0:T(8,128)(2,1)S(1)}, u32[]{:S(2)}, u32[]{:S(2)}) collective-permute-start(bf16[64,1024]{1,0:T(8,128)(2,1)S(1)} %copy-done.4), channel_id=1, source_target_pairs={{0,4},{1,5},{2,6},{3,7},{4,8},{5,9},{6,10},{7,11},{8,12},{9,13},{1... | collective-permute-start | bytes 393224 | tf_op jit(solution)/shard_map/ppermute | solution.py:449
  8.6 2.5 %first_weights.1 = (bf16[128,1024]{1,0:T(8,128)(2,1)}, bf16[128,1024]{1,0:T(8,128)(2,1)}, bf16[384,768]{1,0:T(8,128)(2,1)}) custom-call(bf16[3,64,1024]{2,1,0:T(8,128)(2,1)} %bitcast.20, bf16[64,1024]{1,0:T(8,128)(2,1)} %o_ref.1, bf16[7,96,100]{2,1,0:T(8,128)(2,1)} %pre_ref.1, bf16[144,768]{1,0:T(8,128)(2,1)} %bitcast.21, bf16[144,768]{1,0:T(8,128)(2,1)} %bitcast.22), custom_call_target="tpu_custom_call" | custom-call | bytes 3145728 | tf_op jit(solution)/shard_map/first_weights/pallas_call | solution.py:433
  12.7 6.4 %collective-permute-done.3.refs_4_ = bf16[64,1024]{1,0:T(8,128)(2,1)S(1)} collective-permute-done((bf16[64,1024]{1,0:T(8,128)(2,1)S(1)}, bf16[64,1024]{1,0:T(8,128)(2,1)S(1)}, u32[]{:S(2)}, u32[]{:S(2)}) %collective-permute-start.3) | collective-permute-done | bytes 131104 | tf_op jit(solution)/shard_map/ppermute | solution.py:449
  21.2 2.9 %collective-permute-done.2.refs_3_ = bf16[64,1024]{1,0:T(8,128)(2,1)S(1)} collective-permute-done((bf16[64,1024]{1,0:T(8,128)(2,1)S(1)}, bf16[64,1024]{1,0:T(8,128)(2,1)S(1)}, u32[]{:S(2)}, u32[]{:S(2)}) %collective-permute-start.2) | collective-permute-done | bytes 131104 | tf_op jit(solution)/shard_map/ppermute | solution.py:485
  26.3 2.5 %shard_map.141 = bf16[16,96,384]{2,1,0:T(8,128)(2,1)} custom-call(bf16[8,96,768]{2,1,0:T(8,128)(2,1)S(1)} %copy-done.1), custom_call_target="tpu_custom_call" | custom-call | bytes 3145728 | tf_op jit(solution)/shard_map/pallas_call | solution.py:43
  28.8 4.5 %all-to-all-start = ((bf16[16,96,384]{2,1,0:T(8,128)(2,1)}), bf16[16,96,384]{2,1,0:T(8,128)(2,1)}, u32[]{:S(2)}, u32[]{:S(2)}) async-start(bf16[16,96,384]{2,1,0:T(8,128)(2,1)} %shard_map.141), calls=%async_computation | async-start | bytes 2359296 | tf_op jit(solution)/shard_map/all_to_all | solution.py:384
  33.3 3.1 %collective-permute-start.28 = (bf16[384,768]{1,0:T(8,128)(2,1)}, bf16[384,768]{1,0:T(8,128)(2,1)S(1)}, u32[]{:S(2)}, u32[]{:S(2)}) collective-permute-start(bf16[384,768]{1,0:T(8,128)(2,1)} %get-tuple-element.35.own), channel_id=1, source_target_pairs={{0,12},{1,13},{2,14},{3,15},{4,0},{5,1},{6,2},{7,3},{8,4},{9,5},{1... | collective-permute-start | bytes 1769480 | tf_op jit(solution)/shard_map/ppermute | solution.py:458
  39.3 2.3 %collective-permute-start.5 = (bf16[64,1024]{1,0:T(8,128)(2,1)S(1)}, bf16[64,1024]{1,0:T(8,128)(2,1)S(1)}, u32[]{:S(2)}, u32[]{:S(2)}) collective-permute-start(bf16[64,1024]{1,0:T(8,128)(2,1)S(1)} %copy-done.18), channel_id=1, source_target_pairs={{0,2},{1,3},{2,0},{3,1},{4,6},{5,7},{6,4},{7,5},{8,10},{9,11},{10,... | collective-permute-start | bytes 393224 | tf_op jit(solution)/shard_map/ppermute | solution.py:486
  41.6 3.8 %collective-permute-done.5.refs_6_ = bf16[64,1024]{1,0:T(8,128)(2,1)S(1)} collective-permute-done((bf16[64,1024]{1,0:T(8,128)(2,1)S(1)}, bf16[64,1024]{1,0:T(8,128)(2,1)S(1)}, u32[]{:S(2)}, u32[]{:S(2)}) %collective-permute-start.5) | collective-permute-done | bytes 131104 | tf_op jit(solution)/shard_map/ppermute | solution.py:486
  46.2 4.8 %collective-permute-done.6.refs_7_ = bf16[64,1024]{1,0:T(8,128)(2,1)S(1)} collective-permute-done((bf16[64,1024]{1,0:T(8,128)(2,1)S(1)}, bf16[64,1024]{1,0:T(8,128)(2,1)S(1)}, u32[]{:S(2)}, u32[]{:S(2)}) %collective-permute-start.6) | collective-permute-done | bytes 131104 | tf_op jit(solution)/shard_map/ppermute | solution.py:486
  51.6 2.9 %collective-permute-start.12 = (bf16[128,1024]{1,0:T(8,128)(2,1)}, bf16[128,1024]{1,0:T(8,128)(2,1)}, u32[]{:S(2)}, u32[]{:S(2)}) collective-permute-start(bf16[128,1024]{1,0:T(8,128)(2,1)} %collective-permute-done.10.refs_13_), channel_id=1, source_target_pairs={{0,12},{1,13},{2,14},{3,15},{4,0},{5,1},{6,2},{7,3},{8,4},{9,5},{1... | collective-permute-start | bytes 786440 | tf_op jit(solution)/shard_map/ppermute | solution.py:455
  55.2 7.0 %collective-permute-done.28.right = bf16[384,768]{1,0:T(8,128)(2,1)S(1)} collective-permute-done((bf16[384,768]{1,0:T(8,128)(2,1)}, bf16[384,768]{1,0:T(8,128)(2,1)S(1)}, u32[]{:S(2)}, u32[]{:S(2)}) %collective-permute-start.28) | collective-permute-done | bytes 589856 | tf_op jit(solution)/shard_map/ppermute | solution.py:458
  67.9 8.9 %attention.1 = (bf16[64,1024]{1,0:T(8,128)(2,1)}, bf16[64,1024]{1,0:T(8,128)(2,1)}, bf16[64,1024]{1,0:T(8,128)(2,1)}, bf16[64,1024]{1,0:T(8,128)(2,1)}) custom-call(s32[1]{0:T(128)} %bitcast.flag_ref, f32[8,1024]{1,0:T(8,128)} %mod_ref.5, bf16[64,1024]{1,0:T(8,128)(2,1)} %frames_ref.1, bf16[64,1024]{1,0:T(8,128)(2,1)} %copy-done.19, ...), custom_call_target="tpu_custom_call" | custom-call | flops 1000000000 | bytes 4194304 | tf_op jit(solution)/shard_map/attention/pallas_call | solution.py:501
  77.0 2.5 %collective-permute-start.14 = (bf16[64,1024]{1,0:T(8,128)(2,1)}, bf16[64,1024]{1,0:T(8,128)(2,1)S(1)}, u32[]{:S(2)}, u32[]{:S(2)}) collective-permute-start(bf16[64,1024]{1,0:T(8,128)(2,1)} %get-tuple-element.26), channel_id=1, source_target_pairs={{0,2},{1,3},{2,0},{3,1},{4,6},{5,7},{6,4},{7,5},{8,10},{9,11},{10,... | collective-permute-start | bytes 393224 | tf_op jit(solution)/shard_map/ppermute | solution.py:534
  79.6 3.2 %voc_merge.1 = (bf16[4,96,768]{2,1,0:T(8,128)(2,1)}, bf16[4,144,768]{2,1,0:T(8,128)(2,1)}, bf16[4,144,768]{2,1,0:T(8,128)(2,1)}) custom-call(bf16[384,768]{1,0:T(8,128)(2,1)} %get-tuple-element.35.own, bf16[384,768]{1,0:T(8,128)(2,1)} %copy-done.9, bf16[384,768]{1,0:T(8,128)(2,1)} %copy-done.10, bf16[240,768]{1,0:T(8,128)(2,1)} %collective-permute-done.29.far_top, ...), custom_call_target="tpu_custom_call" | custom-call | bytes 5242880 | tf_op jit(solution)/shard_map/voc_merge/pallas_call | solution.py:463
  84.0 2.2 %collective-permute-done.15.p3 = bf16[64,1024]{1,0:T(8,128)(2,1)S(1)} collective-permute-done((bf16[64,1024]{1,0:T(8,128)(2,1)}, bf16[64,1024]{1,0:T(8,128)(2,1)S(1)}, u32[]{:S(2)}, u32[]{:S(2)}) %collective-permute-start.15) | collective-permute-done | bytes 131104 | tf_op jit(solution)/shard_map/ppermute | solution.py:534
  86.5 2.8 %collective-permute-start.16 = (bf16[64,1024]{1,0:T(8,128)(2,1)S(1)}, bf16[64,1024]{1,0:T(8,128)(2,1)S(1)}, u32[]{:S(2)}, u32[]{:S(2)}) collective-permute-start(bf16[64,1024]{1,0:T(8,128)(2,1)S(1)} %get-tuple-element.29.h0), channel_id=1, source_target_pairs={{0,8},{1,9},{2,10},{3,11},{4,12},{5,13},{6,14},{7,15},{8,0},{9,1},... | collective-permute-start | bytes 393224 | tf_op jit(solution)/shard_map/ppermute | solution.py:546
  89.3 3.2 %collective-permute-start.18 = (bf16[64,1024]{1,0:T(8,128)(2,1)S(1)}, bf16[64,1024]{1,0:T(8,128)(2,1)S(1)}, u32[]{:S(2)}, u32[]{:S(2)}) collective-permute-start(bf16[64,1024]{1,0:T(8,128)(2,1)S(1)} %get-tuple-element.29.h0), channel_id=1, source_target_pairs={{0,12},{1,13},{2,14},{3,15},{4,0},{5,1},{6,2},{7,3},{8,4},{9,5},{1... | collective-permute-start | bytes 393224 | tf_op jit(solution)/shard_map/ppermute | solution.py:548
  98.1 3.1 %shard_map.143 = (bf16[64,1024]{1,0:T(8,128)(2,1)S(1)}, bf16[64,1024]{1,0:T(8,128)(2,1)S(1)}, bf16[64,1024]{1,0:T(8,128)(2,1)S(1)}, bf16[64,1024]{1,0:T(8,128)(2,1)S(1)}) custom-call(bf16[64,1024]{1,0:T(8,128)(2,1)S(1)} %get-tuple-element.29.h0, bf16[64,1024]{1,0:T(8,128)(2,1)S(1)} %collective-permute-done.16.h1, ...), custom_call_target="tpu_custom_call" | custom-call | flops 1100000000 | bytes 5242880 | tf_op jit(solution)/shard_map/pallas_call | solution.py:43
  105.3 2.5 %collective-permute-done.22.p1 = bf16[64,1024]{1,0:T(8,128)(2,1)S(1)} collective-permute-done((bf16[64,1024]{1,0:T(8,128)(2,1)S(1)}, bf16[64,1024]{1,0:T(8,128)(2,1)S(1)}, u32[]{:S(2)}, u32[]{:S(2)}) %collective-permute-start.22) | collective-permute-done | bytes 131104 | tf_op jit(solution)/shard_map/ppermute | solution.py:559
  107.8 2.5 %collective-permute-start.24 = (bf16[64,1024]{1,0:T(8,128)(2,1)S(1)}, bf16[64,1024]{1,0:T(8,128)(2,1)S(1)}, u32[]{:S(2)}, u32[]{:S(2)}) collective-permute-start(bf16[64,1024]{1,0:T(8,128)(2,1)S(1)} %get-tuple-element.33), channel_id=1, source_target_pairs={{0,4},{1,5},{2,6},{3,7},{4,8},{5,9},{6,10},{7,11},{8,12},{9,13},{1... | collective-permute-start | bytes 393224 | tf_op jit(solution)/shard_map/ppermute | solution.py:561
  110.7 3.3 %collective-permute-done.24.p3 = bf16[64,1024]{1,0:T(8,128)(2,1)S(1)} collective-permute-done((bf16[64,1024]{1,0:T(8,128)(2,1)S(1)}, bf16[64,1024]{1,0:T(8,128)(2,1)S(1)}, u32[]{:S(2)}, u32[]{:S(2)}) %collective-permute-start.24) | collective-permute-done | bytes 131104 | tf_op jit(solution)/shard_map/ppermute | solution.py:561
  115.2 3.6 %all-to-all-start.1 = ((f32[16,64,100]{2,1,0:T(8,128)}), f32[16,64,100]{2,1,0:T(8,128)S(1)}, u32[]{:S(2)}, u32[]{:S(2)}) async-start(f32[16,64,100]{2,1,0:T(8,128)} %shard_map.144), calls=%async_computation.1 | async-start | bytes 1048576 | tf_op jit(solution)/shard_map/all_to_all | solution.py:384
  120.2 9.4 %all-to-all-done.1.mel_ref = f32[16,64,100]{2,1,0:T(8,128)S(1)} async-done(((f32[16,64,100]{2,1,0:T(8,128)}), f32[16,64,100]{2,1,0:T(8,128)S(1)}, u32[]{:S(2)}, u32[]{:S(2)}) %all-to-all-start.1) | async-done | bytes 409632 | tf_op jit(solution)/shard_map/all_to_all | solution.py:384
  132.3 3.9 %prelude_weights.1 = bf16[16,96,768]{2,1,0:T(8,128)(2,1)} custom-call(s32[2]{0:T(128)} %pad_add_fusion.place_ref, bf16[4,96,768]{2,1,0:T(8,128)(2,1)} %get-tuple-element.36.p0, bf16[4,96,768]{2,1,0:T(8,128)(2,1)} %copy-done.13, bf16[4,96,768]{2,1,0:T(8,128)(2,1)} %collective-permute-done.32.p2, bf16[4,96,768]{2,1,0:T(8,128)(2,1)} %collective-permute-done.33.p3), custom_call_target="tpu_custom_call" | custom-call | bytes 5242880 | tf_op jit(solution)/shard_map/prelude_weights/pallas_call | solution.py:573
  136.2 3.2 %collective-permute-done.25.before_ref = f32[8,100]{1,0:T(8,128)S(1)} collective-permute-done((f32[8,100]{1,0:T(8,128)S(1)}, f32[8,100]{1,0:T(8,128)S(1)}, u32[]{:S(2)}, u32[]{:S(2)}) %collective-permute-start.25) | collective-permute-done | bytes 3232 | tf_op jit(solution)/shard_map/ppermute | solution.py:593
  139.4 4.3 %collective-permute-start.26 = (f32[8,100]{1,0:T(8,128)S(1)}, f32[8,100]{1,0:T(8,128)S(1)}, u32[]{:S(2)}, u32[]{:S(2)}) collective-permute-start(f32[8,100]{1,0:T(8,128)S(1)} %get-tuple-element.44), channel_id=1, source_target_pairs={{16,0},{32,16},{48,32},{64,48},{80,64},{96,80},{112,96},{128,112},... | collective-permute-start | bytes 9608 | tf_op jit(solution)/shard_map/ppermute | solution.py:594
  143.8 3.4 %convolution_bitcast_fusion.comp_ref = f32[768,384]{1,0:T(8,128)S(1)} fusion(bf16[16,96,768]{2,1,0:T(8,128)(2,1)} %prelude_weights.1, bf16[16,96,384]{2,1,0:T(8,128)(2,1)} %all-to-all-done), kind=kOutput, calls=%fused_computation | convolution fusion | flops 905969664 | bytes 4718592 | tf_op jit(solution)/shard_map/dot_general | solution.py:583
  147.5 2.5 %shard_map.146 = bf16[16,72,192]{2,1,0:T(8,128)(2,1)} custom-call(s32[2]{0:T(128)S(1)} %add_convert_fusion.1.flag_ref, f32[16,64,100]{2,1,0:T(8,128)S(1)} %all-to-all-done.1.mel_ref, f32[8,100]{1,0:T(8,128)S(1)} %collective-permute-done.25.before_ref, f32[8,100]{1,0:T(8,128)S(1)} %collective-permute-done.26.after_ref, ...), custom_call_target="tpu_custom_call" | custom-call | flops 500000000 | bytes 2097152 | tf_op jit(solution)/shard_map/pallas_call | solution.py:43
  150.0 3.6 %all-to-all-start.2 = ((bf16[16,72,192]{2,1,0:T(8,128)(2,1)}), bf16[16,72,192]{2,1,0:T(8,128)(2,1)S(1)}, u32[]{:S(2)}, u32[]{:S(2)}) async-start(bf16[16,72,192]{2,1,0:T(8,128)(2,1)} %shard_map.146), calls=%async_computation.2 | async-start | bytes 1179648 | tf_op jit(solution)/shard_map/all_to_all | solution.py:384
  155.2 9.8 %all-to-all-done.2.up_ref = bf16[16,72,192]{2,1,0:T(8,128)(2,1)S(1)} async-done(((bf16[16,72,192]{2,1,0:T(8,128)(2,1)}), bf16[16,72,192]{2,1,0:T(8,128)(2,1)S(1)}, u32[]{:S(2)}, u32[]{:S(2)}) %all-to-all-start.2) | async-done | bytes 442400 | tf_op jit(solution)/shard_map/all_to_all | solution.py:384
  165.9 8.3 %convolutions.1 = bf16[64,3072]{1,0:T(8,128)(2,1)} custom-call(s32[2]{0:T(128)} %add_convert_fusion.flag_ref, s32[2]{0:T(128)} %pad_add_fusion.place_ref, bf16[16,72,192]{2,1,0:T(8,128)(2,1)} %copy-done.8, f32[2,768]{1,0:T(2,128)} %alpha_ref.1, bf16[4,144,768]{2,1,0:T(8,128)(2,1)} %get-tuple-element.40.refs_0_, bf16[4,144,768]{2,1,0:T(8,128)(2,1)} %copy-done.12, ...), custom_call_target="tpu_custom_call" | custom-call | flops 2000000000 | bytes 8388608 | tf_op jit(solution)/shard_map/convolutions/pallas_call | solution.py:613
  (128 shorter events, 42.7 us)
Async XLA Ops:
  2.9 34.0 %collective-permute-start.20 = (bf16[2048,256]{1,0:T(8,128)(2,1)S(1)}, bf16[2048,256]{1,0:T(8,128)(2,1)}, u32[]{:S(2)}, u32[]{:S(2)}) collective-permute-start(bf16[2048,256]{1,0:T(8,128)(2,1)S(1)} %shard_map.142.w0), channel_id=1, source_target_pairs={{0,130},{1,131},{2,128},{3,129},{4,134},{5,135},{6,132},{7,133},{8... | collective-permute-start | bytes 3145736 | tf_op jit(solution)/shard_map/ppermute | solution.py:492
  3.8 15.3 %collective-permute-start.3 = (bf16[64,1024]{1,0:T(8,128)(2,1)S(1)}, bf16[64,1024]{1,0:T(8,128)(2,1)S(1)}, u32[]{:S(2)}, u32[]{:S(2)}) collective-permute-start(bf16[64,1024]{1,0:T(8,128)(2,1)S(1)} %copy-done.4), channel_id=1, source_target_pairs={{0,4},{1,5},{2,6},{3,7},{4,8},{5,9},{6,10},{7,11},{8,12},{9,13},{1... | collective-permute-start | bytes 393224 | tf_op jit(solution)/shard_map/ppermute | solution.py:449
  7.2 12.0 %collective-permute-start = (bf16[64,1024]{1,0:T(8,128)(2,1)S(1)}, bf16[64,1024]{1,0:T(8,128)(2,1)S(1)}, u32[]{:S(2)}, u32[]{:S(2)}) collective-permute-start(bf16[64,1024]{1,0:T(8,128)(2,1)S(1)} %copy-done.4), channel_id=1, source_target_pairs={{0,1},{1,0},{2,3},{3,2},{4,5},{5,4},{6,7},{7,6},{8,9},{9,8},{10,11... | collective-permute-start | bytes 393224 | tf_op jit(solution)/shard_map/ppermute | solution.py:485
  7.3 12.0 %collective-permute-start.1 = (bf16[64,1024]{1,0:T(8,128)(2,1)S(1)}, bf16[64,1024]{1,0:T(8,128)(2,1)S(1)}, u32[]{:S(2)}, u32[]{:S(2)}) collective-permute-start(bf16[64,1024]{1,0:T(8,128)(2,1)S(1)} %copy-done.4), channel_id=1, source_target_pairs={{0,2},{1,3},{2,0},{3,1},{4,6},{5,7},{6,4},{7,5},{8,10},{9,11},{10,... | collective-permute-start | bytes 393224 | tf_op jit(solution)/shard_map/ppermute | solution.py:485
  11.2 13.0 %collective-permute-start.7 = (bf16[128,1024]{1,0:T(8,128)(2,1)}, bf16[128,1024]{1,0:T(8,128)(2,1)S(1)}, u32[]{:S(2)}, u32[]{:S(2)}) collective-permute-start(bf16[128,1024]{1,0:T(8,128)(2,1)} %get-tuple-element.22.refs_8_), channel_id=1, source_target_pairs={{0,4},{1,5},{2,6},{3,7},{4,8},{5,9},{6,10},{7,11},{8,12},{9,13},{1... | collective-permute-start | bytes 786440 | tf_op jit(solution)/shard_map/ppermute | solution.py:450
  19.1 14.2 %collective-permute-start.10 = (bf16[128,1024]{1,0:T(8,128)(2,1)}, bf16[128,1024]{1,0:T(8,128)(2,1)}, u32[]{:S(2)}, u32[]{:S(2)}) collective-permute-start(bf16[128,1024]{1,0:T(8,128)(2,1)} %get-tuple-element.23.refs_9_), channel_id=1, source_target_pairs={{0,12},{1,13},{2,14},{3,15},{4,0},{5,1},{6,2},{7,3},{8,4},{9,5},{1... | collective-permute-start | bytes 786440 | tf_op jit(solution)/shard_map/ppermute | solution.py:451
  19.2 17.2 %collective-permute-start.8 = (bf16[128,1024]{1,0:T(8,128)(2,1)}, bf16[128,1024]{1,0:T(8,128)(2,1)}, u32[]{:S(2)}, u32[]{:S(2)}) collective-permute-start(bf16[128,1024]{1,0:T(8,128)(2,1)} %get-tuple-element.23.refs_9_), channel_id=1, source_target_pairs={{0,4},{1,5},{2,6},{3,7},{4,8},{5,9},{6,10},{7,11},{8,12},{9,13},{1... | collective-permute-start | bytes 786440 | tf_op jit(solution)/shard_map/ppermute | solution.py:452
  24.2 12.3 %collective-permute-start.9 = (bf16[128,1024]{1,0:T(8,128)(2,1)}, bf16[128,1024]{1,0:T(8,128)(2,1)}, u32[]{:S(2)}, u32[]{:S(2)}) collective-permute-start(bf16[128,1024]{1,0:T(8,128)(2,1)} %get-tuple-element.22.refs_8_), channel_id=1, source_target_pairs={{0,12},{1,13},{2,14},{3,15},{4,0},{5,1},{6,2},{7,3},{8,4},{9,5},{1... | collective-permute-start | bytes 786440 | tf_op jit(solution)/shard_map/ppermute | solution.py:453
  24.8 26.1 %collective-permute-start.27 = (bf16[384,768]{1,0:T(8,128)(2,1)}, bf16[384,768]{1,0:T(8,128)(2,1)S(1)}, u32[]{:S(2)}, u32[]{:S(2)}) collective-permute-start(bf16[384,768]{1,0:T(8,128)(2,1)} %get-tuple-element.35.own), channel_id=1, source_target_pairs={{0,4},{1,5},{2,6},{3,7},{4,8},{5,9},{6,10},{7,11},{8,12},{9,13},{1... | collective-permute-start | bytes 1769480 | tf_op jit(solution)/shard_map/ppermute | solution.py:457
  28.8 57.7 %all-to-all-start = ((bf16[16,96,384]{2,1,0:T(8,128)(2,1)}), bf16[16,96,384]{2,1,0:T(8,128)(2,1)}, u32[]{:S(2)}, u32[]{:S(2)}) async-start(bf16[16,96,384]{2,1,0:T(8,128)(2,1)} %shard_map.141), calls=%async_computation | async-start | bytes 2359296 | tf_op jit(solution)/shard_map/all_to_all | solution.py:384
  33.3 28.9 %collective-permute-start.28 = (bf16[384,768]{1,0:T(8,128)(2,1)}, bf16[384,768]{1,0:T(8,128)(2,1)S(1)}, u32[]{:S(2)}, u32[]{:S(2)}) collective-permute-start(bf16[384,768]{1,0:T(8,128)(2,1)} %get-tuple-element.35.own), channel_id=1, source_target_pairs={{0,12},{1,13},{2,14},{3,15},{4,0},{5,1},{6,2},{7,3},{8,4},{9,5},{1... | collective-permute-start | bytes 1769480 | tf_op jit(solution)/shard_map/ppermute | solution.py:458
  36.5 52.8 %collective-permute-start.19 = (bf16[2048,256]{1,0:T(8,128)(2,1)S(1)}, bf16[2048,256]{1,0:T(8,128)(2,1)S(1)}, u32[]{:S(2)}, u32[]{:S(2)}) collective-permute-start(bf16[2048,256]{1,0:T(8,128)(2,1)S(1)} %shard_map.142.w0), channel_id=1, source_target_pairs={{0,1},{1,0},{2,3},{3,2},{4,5},{5,4},{6,7},{7,6},{8,9},{9,8},{10,11... | collective-permute-start | bytes 3145736 | tf_op jit(solution)/shard_map/ppermute | solution.py:491
  37.0 61.2 %collective-permute-start.21 = (bf16[2048,256]{1,0:T(8,128)(2,1)}, bf16[2048,256]{1,0:T(8,128)(2,1)}, u32[]{:S(2)}, u32[]{:S(2)}) collective-permute-start(bf16[2048,256]{1,0:T(8,128)(2,1)} %collective-permute-done.20.w2), channel_id=1, source_target_pairs={{0,1},{1,0},{2,3},{3,2},{4,5},{5,4},{6,7},{7,6},{8,9},{9,8},{10,11... | collective-permute-start | bytes 3145736 | tf_op jit(solution)/shard_map/ppermute | solution.py:493
  50.9 13.4 %collective-permute-start.11 = (bf16[128,1024]{1,0:T(8,128)(2,1)S(1)}, bf16[128,1024]{1,0:T(8,128)(2,1)S(1)}, u32[]{:S(2)}, u32[]{:S(2)}) collective-permute-start(bf16[128,1024]{1,0:T(8,128)(2,1)S(1)} %collective-permute-done.7.refs_10_), channel_id=1, source_target_pairs={{0,4},{1,5},{2,6},{3,7},{4,8},{5,9},{6,10},{7,11},{8,12},{9,13},{1... | collective-permute-start | bytes 786440 | tf_op jit(solution)/shard_map/ppermute | solution.py:454
  51.6 16.4 %collective-permute-start.12 = (bf16[128,1024]{1,0:T(8,128)(2,1)}, bf16[128,1024]{1,0:T(8,128)(2,1)}, u32[]{:S(2)}, u32[]{:S(2)}) collective-permute-start(bf16[128,1024]{1,0:T(8,128)(2,1)} %collective-permute-done.10.refs_13_), channel_id=1, source_target_pairs={{0,12},{1,13},{2,14},{3,15},{4,0},{5,1},{6,2},{7,3},{8,4},{9,5},{1... | collective-permute-start | bytes 786440 | tf_op jit(solution)/shard_map/ppermute | solution.py:455
  62.2 17.2 %collective-permute-start.29 = (bf16[240,768]{1,0:T(8,128)(2,1)}, bf16[240,768]{1,0:T(8,128)(2,1)}, u32[]{:S(2)}, u32[]{:S(2)}) collective-permute-start(bf16[240,768]{1,0:T(8,128)(2,1)} %slice.18), channel_id=1, source_target_pairs={{0,4},{1,5},{2,6},{3,7},{4,8},{5,9},{6,10},{7,11},{8,12},{9,13},{1... | collective-permute-start | bytes 1105928 | tf_op jit(solution)/shard_map/ppermute | solution.py:459
  65.0 11.9 %collective-permute-start.30 = (bf16[144,768]{1,0:T(8,128)(2,1)}, bf16[144,768]{1,0:T(8,128)(2,1)}, u32[]{:S(2)}, u32[]{:S(2)}) collective-permute-start(bf16[144,768]{1,0:T(8,128)(2,1)} %slice.19), channel_id=1, source_target_pairs={{0,12},{1,13},{2,14},{3,15},{4,0},{5,1},{6,2},{7,3},{8,4},{9,5},{1... | collective-permute-start | bytes 663560 | tf_op jit(solution)/shard_map/ppermute | solution.py:460
  82.8 36.3 %collective-permute-start.32 = (bf16[4,96,768]{2,1,0:T(8,128)(2,1)}, bf16[4,96,768]{2,1,0:T(8,128)(2,1)}, u32[]{:S(2)}, u32[]{:S(2)}) collective-permute-start(bf16[4,96,768]{2,1,0:T(8,128)(2,1)} %get-tuple-element.36.p0), channel_id=1, source_target_pairs={{0,130},{1,131},{2,128},{3,129},{4,134},{5,135},{6,132},{7,133},{8... | collective-permute-start | bytes 1769480 | tf_op jit(solution)/shard_map/ppermute | solution.py:474
  86.5 8.0 %collective-permute-start.16 = (bf16[64,1024]{1,0:T(8,128)(2,1)S(1)}, bf16[64,1024]{1,0:T(8,128)(2,1)S(1)}, u32[]{:S(2)}, u32[]{:S(2)}) collective-permute-start(bf16[64,1024]{1,0:T(8,128)(2,1)S(1)} %get-tuple-element.29.h0), channel_id=1, source_target_pairs={{0,8},{1,9},{2,10},{3,11},{4,12},{5,13},{6,14},{7,15},{8,0},{9,1},... | collective-permute-start | bytes 393224 | tf_op jit(solution)/shard_map/ppermute | solution.py:546
  89.3 8.9 %collective-permute-start.18 = (bf16[64,1024]{1,0:T(8,128)(2,1)S(1)}, bf16[64,1024]{1,0:T(8,128)(2,1)S(1)}, u32[]{:S(2)}, u32[]{:S(2)}) collective-permute-start(bf16[64,1024]{1,0:T(8,128)(2,1)S(1)} %get-tuple-element.29.h0), channel_id=1, source_target_pairs={{0,12},{1,13},{2,14},{3,15},{4,0},{5,1},{6,2},{7,3},{8,4},{9,5},{1... | collective-permute-start | bytes 393224 | tf_op jit(solution)/shard_map/ppermute | solution.py:548
  94.4 35.3 %collective-permute-start.35 = (bf16[4,144,768]{2,1,0:T(8,128)(2,1)}, bf16[4,144,768]{2,1,0:T(8,128)(2,1)}, u32[]{:S(2)}, u32[]{:S(2)}) collective-permute-start(bf16[4,144,768]{2,1,0:T(8,128)(2,1)} %get-tuple-element.40.refs_0_), channel_id=1, source_target_pairs={{0,130},{1,131},{2,128},{3,129},{4,134},{5,135},{6,132},{7,133},{8... | collective-permute-start | bytes 2654216 | tf_op jit(solution)/shard_map/ppermute | solution.py:475
  96.5 33.7 %collective-permute-start.38 = (bf16[4,144,768]{2,1,0:T(8,128)(2,1)}, bf16[4,144,768]{2,1,0:T(8,128)(2,1)}, u32[]{:S(2)}, u32[]{:S(2)}) collective-permute-start(bf16[4,144,768]{2,1,0:T(8,128)(2,1)} %get-tuple-element.41.refs_4_), channel_id=1, source_target_pairs={{0,2},{1,3},{2,0},{3,1},{4,6},{5,7},{6,4},{7,5},{8,10},{9,11},{10,... | collective-permute-start | bytes 2654216 | tf_op jit(solution)/shard_map/ppermute | solution.py:476
  115.2 14.4 %all-to-all-start.1 = ((f32[16,64,100]{2,1,0:T(8,128)}), f32[16,64,100]{2,1,0:T(8,128)S(1)}, u32[]{:S(2)}, u32[]{:S(2)}) async-start(f32[16,64,100]{2,1,0:T(8,128)} %shard_map.144), calls=%async_computation.1 | async-start | bytes 1048576 | tf_op jit(solution)/shard_map/all_to_all | solution.py:384
  118.8 10.8 %collective-permute-start.31 = (bf16[4,96,768]{2,1,0:T(8,128)(2,1)}, bf16[4,96,768]{2,1,0:T(8,128)(2,1)S(1)}, u32[]{:S(2)}, u32[]{:S(2)}) collective-permute-start(bf16[4,96,768]{2,1,0:T(8,128)(2,1)} %get-tuple-element.36.p0), channel_id=1, source_target_pairs={{0,1},{1,0},{2,3},{3,2},{4,5},{5,4},{6,7},{7,6},{8,9},{9,8},{10,11... | collective-permute-start | bytes 1769480 | tf_op jit(solution)/shard_map/ppermute | solution.py:477
  119.1 11.2 %collective-permute-start.33 = (bf16[4,96,768]{2,1,0:T(8,128)(2,1)}, bf16[4,96,768]{2,1,0:T(8,128)(2,1)}, u32[]{:S(2)}, u32[]{:S(2)}) collective-permute-start(bf16[4,96,768]{2,1,0:T(8,128)(2,1)} %collective-permute-done.32.p2), channel_id=1, source_target_pairs={{0,1},{1,0},{2,3},{3,2},{4,5},{5,4},{6,7},{7,6},{8,9},{9,8},{10,11... | collective-permute-start | bytes 1769480 | tf_op jit(solution)/shard_map/ppermute | solution.py:480
  120.0 35.2 %collective-permute-start.34 = (bf16[4,144,768]{2,1,0:T(8,128)(2,1)S(1)}, bf16[4,144,768]{2,1,0:T(8,128)(2,1)S(1)}, u32[]{:S(2)}, u32[]{:S(2)}) collective-permute-start(bf16[4,144,768]{2,1,0:T(8,128)(2,1)S(1)} %copy-done.11), channel_id=1, source_target_pairs={{0,1},{1,0},{2,3},{3,2},{4,5},{5,4},{6,7},{7,6},{8,9},{9,8},{10,11... | collective-permute-start | bytes 2654216 | tf_op jit(solution)/shard_map/ppermute | solution.py:478
  129.6 25.6 %collective-permute-start.37 = (bf16[4,144,768]{2,1,0:T(8,128)(2,1)}, bf16[4,144,768]{2,1,0:T(8,128)(2,1)}, u32[]{:S(2)}, u32[]{:S(2)}) collective-permute-start(bf16[4,144,768]{2,1,0:T(8,128)(2,1)} %get-tuple-element.41.refs_4_), channel_id=1, source_target_pairs={{0,1},{1,0},{2,3},{3,2},{4,5},{5,4},{6,7},{7,6},{8,9},{9,8},{10,11... | collective-permute-start | bytes 2654216 | tf_op jit(solution)/shard_map/ppermute | solution.py:479
  129.7 25.5 %collective-permute-start.36 = (bf16[4,144,768]{2,1,0:T(8,128)(2,1)}, bf16[4,144,768]{2,1,0:T(8,128)(2,1)}, u32[]{:S(2)}, u32[]{:S(2)}) collective-permute-start(bf16[4,144,768]{2,1,0:T(8,128)(2,1)} %collective-permute-done.35.refs_2_), channel_id=1, source_target_pairs={{0,1},{1,0},{2,3},{3,2},{4,5},{5,4},{6,7},{7,6},{8,9},{9,8},{10,11... | collective-permute-start | bytes 2654216 | tf_op jit(solution)/shard_map/ppermute | solution.py:481
  130.2 25.0 %collective-permute-start.39 = (bf16[4,144,768]{2,1,0:T(8,128)(2,1)}, bf16[4,144,768]{2,1,0:T(8,128)(2,1)}, u32[]{:S(2)}, u32[]{:S(2)}) collective-permute-start(bf16[4,144,768]{2,1,0:T(8,128)(2,1)} %collective-permute-done.38.refs_6_), channel_id=1, source_target_pairs={{0,1},{1,0},{2,3},{3,2},{4,5},{5,4},{6,7},{7,6},{8,9},{9,8},{10,11... | collective-permute-start | bytes 2654216 | tf_op jit(solution)/shard_map/ppermute | solution.py:482
  130.3 9.1 %collective-permute-start.25 = (f32[8,100]{1,0:T(8,128)S(1)}, f32[8,100]{1,0:T(8,128)S(1)}, u32[]{:S(2)}, u32[]{:S(2)}) collective-permute-start(f32[8,100]{1,0:T(8,128)S(1)} %get-tuple-element.45), channel_id=1, source_target_pairs={{0,16},{16,32},{32,48},{48,64},{64,80},{80,96},{96,112},{112,128},... | collective-permute-start | bytes 9608 | tf_op jit(solution)/shard_map/ppermute | solution.py:593
  139.4 8.1 %collective-permute-start.26 = (f32[8,100]{1,0:T(8,128)S(1)}, f32[8,100]{1,0:T(8,128)S(1)}, u32[]{:S(2)}, u32[]{:S(2)}) collective-permute-start(f32[8,100]{1,0:T(8,128)S(1)} %get-tuple-element.44), channel_id=1, source_target_pairs={{16,0},{32,16},{48,32},{64,48},{80,64},{96,80},{112,96},{128,112},... | collective-permute-start | bytes 9608 | tf_op jit(solution)/shard_map/ppermute | solution.py:594
  150.0 15.1 %all-to-all-start.2 = ((bf16[16,72,192]{2,1,0:T(8,128)(2,1)}), bf16[16,72,192]{2,1,0:T(8,128)(2,1)S(1)}, u32[]{:S(2)}, u32[]{:S(2)}) async-start(bf16[16,72,192]{2,1,0:T(8,128)(2,1)} %shard_map.146), calls=%async_computation.2 | async-start | bytes 1179648 | tf_op jit(solution)/shard_map/all_to_all | solution.py:384
  (36 other events, 358.6 us)
